TPU v7x, 32 devices: a whole 2x2x4 slice. The times are simulated.
32 devices in a mesh: chain: 2 (over y), px: 8 (over z, x), py: 2 (over core).
Axes of the slice: x: 2, y: 2, z: 4, core: 2. Of those that a mesh axis runs over, the one named last changes fastest.
Arguments:
- adjoint: float32 [512, 256, 256], P(('chain', 'px'), 'py'), parts along dimension 0, may hold values from -6 to 6
- saved: float32 [512, 256, 256], P(('chain', 'px'), 'py'), parts along dimension 0, may hold values from -6 to 6
- spectra: bfloat16 [2, 256, 256, 256], P(None, None, 'px'), may hold values from -6 to 6, as said below
- freq_index: int32 [8], replicated, may hold values from 1 to 8
- picked: int32 [2], replicated, may hold values from 0 to 7
Outputs:
- force: float32 [512, 256, 256], P(('chain', 'px'), 'py'), parts along dimension 0
There are 2 independent parts, one for each index of `chain`. A program takes and returns all parts, laid end to end along the dimension named above; an argument that names none is the same for every part. Nothing has to cross between parts.
Inputs may be any that keep to these rules, and one draw needn't show every extreme that they name: Each kernel is even in every momentum coordinate separately: spectra[j][k1, k2, k3] is unchanged when k1 is replaced by (256 - k1) mod 256, and likewise k2 with 256 and k3 with 256.
All inputs are finite; a program needn't handle non-finite values.
Results may differ from a plain program's by a relative error of at most 0.0003.
Values sent between devices are 32-bit elements; how exact they have to be, the bound alone decides.
A program may use at most 128 MiB of HBM per device.

v0:
```python
import math

import jax
import jax.numpy as jnp
from jax import lax
from jax.sharding import PartitionSpec as P

L1 = 256
L2 = 256
L3 = 256


def tables(length):
    counter = jnp.arange(length, dtype=jnp.int32)
    product = counter[:, None] * counter[None, :] % length
    angle = product.astype(jnp.float32) * (2.0 * math.pi / length)
    return (jnp.cos(angle), jnp.sin(angle))


def half_tables(length):
    cosine, sine = tables(length)
    half_width = length // 2
    counter = jnp.arange(length, dtype=jnp.int32)
    parity = (1 - 2 * (counter % 2)).astype(jnp.float32)
    first_column = jnp.arange(half_width, dtype=jnp.int32) == 0
    forward_real = cosine[:, :half_width]
    forward_imag = jnp.where(first_column[None, :], parity[:, None], -sine[:, :half_width])
    inverse_real = jnp.where(first_column[:, None], 1.0, 2.0 * cosine[:half_width, :])
    inverse_imag = jnp.where(first_column[:, None], parity[None, :], -2.0 * sine[:half_width, :])
    return (forward_real, forward_imag, inverse_real, inverse_imag)


def reflect(field, axis):
    return jnp.roll(jnp.flip(field, axis), 1, axis)


def along(field, table, axis):
    letters = "abcdef"[: field.ndim]
    result = letters[:axis] + "z" + letters[axis + 1 :]
    return jnp.einsum(
        letters + "," + letters[axis] + "z->" + result,
        field,
        table,
        precision=lax.Precision.HIGHEST,
    )


def rotate(pair, axis, cosine, sine, forward):
    with_cos = along(pair, cosine, axis)
    with_sin = along(pair, sine, axis)
    if forward:
        return jnp.stack([with_cos[0] + with_sin[1], with_cos[1] - with_sin[0]])
    return jnp.stack([with_cos[0] - with_sin[1], with_cos[1] + with_sin[0]])


def on_device(adjoint, saved, spectra, freq_index, picked):
    width_py = lax.axis_size("py")
    py_index = lax.axis_index("py")
    px_index = lax.axis_index("px")
    cos_one, sin_one = tables(L1)
    cos_two, sin_two = tables(L2)
    half_width = L3 // 2
    forward_real, forward_imag, inverse_real, inverse_imag = half_tables(L3)
    real_part = along(adjoint, forward_real, 2)
    imag_part = along(adjoint, forward_imag, 2)
    column_count = half_width // width_py
    columns = lax.all_to_all(
        jnp.stack([real_part, imag_part]), "py", split_axis=3, concat_axis=2, tiled=True
    )
    columns = rotate(columns, 2, cos_two, sin_two, True)
    leading_column = jnp.arange(column_count, dtype=jnp.int32) == 0
    first_slot = leading_column & (py_index == 0)
    slot_ids = jnp.arange(L2, dtype=jnp.int32)
    lower_half = (slot_ids > 0) & (slot_ids < L2 // 2)
    upper_half = slot_ids > L2 // 2
    special = columns[:, :, :, 0]
    mirror = reflect(special, 2)
    packed_real = jnp.where(
        lower_half,
        (special[0] + mirror[0]) * 0.5,
        jnp.where(upper_half, (special[1] + mirror[1]) * 0.5, special[0]),
    )
    packed_imag = jnp.where(
        lower_half,
        (special[1] - mirror[1]) * 0.5,
        jnp.where(upper_half, (mirror[0] - special[0]) * 0.5, special[1]),
    )
    columns = jnp.where(first_slot, jnp.stack([packed_real, packed_imag])[..., None], columns)
    spectral = rotate(
        lax.all_to_all(columns, "px", split_axis=2, concat_axis=1, tiled=True),
        1,
        cos_one,
        sin_one,
        True,
    )
    kernels_all = spectra.astype(jnp.float32)
    local_width = spectra.shape[2]
    global_slots = px_index * local_width + jnp.arange(local_width, dtype=jnp.int32)
    lower_local = (global_slots > 0) & (global_slots < L2 // 2)
    upper_local = global_slots > L2 // 2
    kernel = lax.dynamic_slice_in_dim(kernels_all, py_index * column_count, column_count, 3)
    nyquist = kernels_all[:, :, :, half_width]
    lowest = kernel[..., 0]
    alpha_column = jnp.where(
        lower_local, lowest, jnp.where(upper_local, nyquist, (lowest + nyquist) * 0.5)
    )
    beta_column = jnp.where(lower_local | upper_local, 0.0, (lowest - nyquist) * 0.5) * jnp.where(
        py_index == 0, 1.0, 0.0
    )
    kernel = jnp.where(first_slot, alpha_column[..., None], kernel)
    spectral_mirror = reflect(spectral[..., 0], 1)
    feature_ids = jnp.arange(freq_index.shape[0], dtype=jnp.int32)
    chosen = jnp.sum(
        jnp.where(feature_ids[None, :] == picked[:, None], freq_index[None, :], 0), axis=1
    )
    omegas = chosen.astype(jnp.float32) * (math.pi / 8.0)
    scale = 1.0 / (L1 * L2 * L3)
    slot_count = picked.shape[0]
    groups = [(index, index + 1) for index in range(slot_count)]
    total = jnp.zeros(saved.shape, jnp.float32)
    for start, stop in groups:
        product = spectral[:, None] * kernel[None, start:stop]
        correction = (
            beta_column[start:stop][None]
            * jnp.stack([spectral_mirror[0], -spectral_mirror[1]])[:, None]
        )
        product = product + jnp.where(leading_column, correction[..., None], 0.0)
        product = rotate(product, 2, cos_one, sin_one, False)
        back = lax.all_to_all(product, "px", split_axis=2, concat_axis=3, tiled=True)
        special = back[..., 0]
        mirror = reflect(special, 3)
        untangled_real = jnp.where(
            lower_half,
            special[0] + mirror[1],
            jnp.where(upper_half, mirror[0] - special[1], special[0]),
        )
        untangled_imag = jnp.where(
            lower_half,
            special[1] + mirror[0],
            jnp.where(upper_half, special[0] - mirror[1], special[1]),
        )
        back = jnp.where(first_slot, jnp.stack([untangled_real, untangled_imag])[..., None], back)
        back = rotate(back, 3, cos_two, sin_two, False)
        back = lax.all_to_all(back, "py", split_axis=3, concat_axis=4, tiled=True)
        fields = (along(back[0], inverse_real, 3) + along(back[1], inverse_imag, 3)) * scale
        omega_grid = omegas[start:stop][:, None, None, None]
        total = total + jnp.sum(omega_grid * jnp.cos(omega_grid * saved[None]) * fields, axis=0)
    return total


def solution(mesh):
    placed = (
        P(("chain", "px"), "py", None),
        P(("chain", "px"), "py", None),
        P(None, None, "px", None),
        P(),
        P(),
    )
    return jax.shard_map(
        on_device,
        mesh=mesh,
        in_specs=placed,
        out_specs=P(("chain", "px"), "py", None),
        check_vma=False,
    )
```

profile of v0, /device:TPU:0, one launch (start us, length us, event | category | flops | bytes accessed | tf_op | source)
XLA Modules:
  0.0 787.8 jit_solution(17898030757995129049)
XLA Ops:
  2.0 6.2 convolution_bitcast_fusion.2
  8.3 4.4 convolution_bitcast_fusion.1
  15.6 7.6 all_to_all.108
  23.2 5.2 copy.561
  28.4 6.4 all_to_all.81
  34.8 8.5 %convolution_bitcast_fusion = f32[2,32,256,64]{2,3,1,0:T(8,128)S(1)} fusion(f32[2,32,256,64]{2,3,1,0:T(8,128)} %all_to_all.81), kind=kOutput, calls=%fused_computation.35 | convolution fusion | flops 3222142976 | bytes 8388608 | tf_op jit(solution)/shard_map/abcd,cz->abzd/dot_general | solution.py:40
  43.4 4.9 fusion.26
  51.7 4.4 slice_add_fusion.5
  62.9 6.6 fusion
  69.5 9.2 %copy.448 = f32[2,32,256,64]{3,1,0,2:T(8,128)} copy(f32[2,32,256,64]{2,0,1,3:T(2,128)} %fusion) | data formatting | bytes 8388608 | tf_op jit(solution)/shard_map/jit(_where)/select_n | solution.py:88
  78.7 9.8 %reshape.449 = f32[8,1,131072]{2,1,0:T(1,128)} reshape(f32[256,2,32,64]{3,2,1,0:T(8,128)} %bitcast.257) | data formatting | bytes 8388608
  88.5 7.6 all-to-all-start.1
  96.1 15.9 %copy.455 = bf16[2,256,32,256]{1,2,3,0:T(8,128)(2,1)} copy(bf16[2,256,32,256]{3,2,1,0:T(8,128)(2,1)} %param.7) | data formatting | bytes 16777216 | tf_op args[2]
  112.0 11.3 %convert_element_type.63 = f32[2,256,32,256]{1,2,3,0:T(8,128)} convert(bf16[2,256,32,256]{1,2,3,0:T(8,128)(2,1)} %copy.455) | non-fusion elementwise | flops 4194304 | bytes 25165824 | tf_op jit(solution)/shard_map/convert_element_type | solution.py:96
  133.5 56.1 %all-to-all-done.1 = f32[8,1,131072]{2,1,0:T(1,128)} async-done(((f32[8,1,131072]{2,1,0:T(1,128)}), f32[8,1,131072]{2,1,0:T(1,128)}, u32[]{:S(2)}, u32[]{:S(2)}) %all-to-all-start.1) | async-done | bytes 4194336 | tf_op jit(solution)/shard_map/all_to_all | solution.py:90
  190.1 14.1 %reduce.6 = f32[8,131072]{1,0:T(8,128)} reduce(f32[8,1,131072]{2,1,0:T(1,128)} %all-to-all-done.1, f32[]{:T(128)} %broadcast.356), dimensions={1}, to_apply=%all_to_all.82.reduce_sub_computation | reduce | bytes 8388612 | tf_op jit(solution)/shard_map/all_to_all | solution.py:90
  204.2 8.7 %reshape.450 = f32[256,2,32,64]{3,2,1,0:T(8,128)} reshape(f32[8,131072]{1,0:T(8,128)} %reduce.6) | data formatting | bytes 8388608
  213.0 13.1 %copy.450 = f32[2,8,32,32,64]{4,3,2,1,0:T(8,128)} copy(f32[2,8,32,32,64]{4,2,0,3,1:T(8,128)} %bitcast.264) | data formatting | bytes 8388608 | tf_op jit(solution)/shard_map/all_to_all | solution.py:90
  226.1 7.8 copy.452
  233.9 7.8 fusion.58
  241.7 4.6 fusion.48
  249.1 5.0 select_add_fusion.1
  254.1 4.7 fusion.56
  258.8 4.6 fusion.46
  267.0 9.2 %copy.459 = f32[2,1,256,32,64]{4,3,0,1,2:T(8,128)} copy(f32[2,1,256,32,64]{2,4,3,0,1:T(8,128)} %pad_maximum_fusion.3) | data formatting | bytes 8388608 | tf_op jit(solution)/shard_map/stack | solution.py:53
  276.2 10.2 %reshape.455 = f32[8,1,131072]{2,1,0:T(1,128)} reshape(f32[256,1,2,32,64]{4,3,2,1,0:T(8,128)} %bitcast.258) | data formatting | bytes 8388608
  286.4 4.6 all-to-all-start.2
  291.0 7.6 fusion.54
  298.7 4.6 fusion.50
  307.0 9.2 %copy.482 = f32[2,1,256,32,64]{4,3,0,1,2:T(8,128)} copy(f32[2,1,256,32,64]{2,4,3,0,1:T(8,128)} %pad_maximum_fusion.5) | data formatting | bytes 8388608 | tf_op jit(solution)/shard_map/stack | solution.py:53
  316.2 9.8 %reshape.451 = f32[8,1,131072]{2,1,0:T(1,128)} reshape(f32[256,1,2,32,64]{4,3,2,1,0:T(8,128)} %bitcast.259) | data formatting | bytes 8388608
  326.0 57.7 %all-to-all-done.2 = f32[8,1,131072]{2,1,0:T(1,128)} async-done(((f32[8,1,131072]{2,1,0:T(1,128)}), f32[8,1,131072]{2,1,0:T(1,128)}, u32[]{:S(2)}, u32[]{:S(2)}) %all-to-all-start.2) | async-done | bytes 4194336 | tf_op jit(solution)/shard_map/all_to_all | solution.py:129
  383.7 4.7 all-to-all-start.4
  389.2 13.7 %reduce.7 = f32[8,131072]{1,0:T(8,128)} reduce(f32[8,1,131072]{2,1,0:T(1,128)} %all-to-all-done.2, f32[]{:T(128)} %broadcast.356), dimensions={1}, to_apply=%all_to_all.86.reduce_sub_computation | reduce | bytes 8388612 | tf_op jit(solution)/shard_map/all_to_all | solution.py:129
  402.9 8.7 %reshape.456 = f32[256,1,2,32,64]{4,3,2,1,0:T(8,128)} reshape(f32[8,131072]{1,0:T(8,128)} %reduce.7) | data formatting | bytes 8388608
  411.7 4.4 copy.460
  423.0 58.0 %all-to-all-done.4 = f32[8,1,131072]{2,1,0:T(1,128)} async-done(((f32[8,1,131072]{2,1,0:T(1,128)}), f32[8,1,131072]{2,1,0:T(1,128)}, u32[]{:S(2)}, u32[]{:S(2)}) %all-to-all-start.4) | async-done | bytes 4194336 | tf_op jit(solution)/shard_map/all_to_all | solution.py:129
  480.9 13.9 %reduce.8 = f32[8,131072]{1,0:T(8,128)} reduce(f32[8,1,131072]{2,1,0:T(1,128)} %all-to-all-done.4, f32[]{:T(128)} %broadcast.356), dimensions={1}, to_apply=%all_to_all.94.reduce_sub_computation | reduce | bytes 8388612 | tf_op jit(solution)/shard_map/all_to_all | solution.py:129
  494.8 8.7 %reshape.452 = f32[256,1,2,32,64]{4,3,2,1,0:T(8,128)} reshape(f32[8,131072]{1,0:T(8,128)} %reduce.8) | data formatting | bytes 8388608
  503.5 4.4 copy.483
  509.4 4.1 fusion.159
  515.1 5.2 copy.537
  520.4 8.6 %copy.466 = f32[2,32,256,64]{2,0,1,3:T(2,128)} copy(f32[2,32,256,64]{3,2,1,0:T(8,128)} %bitcast.247) | data formatting | bytes 8388608 | tf_op jit(solution)/shard_map/all_to_all | solution.py:129
  529.4 8.7 %copy.490 = f32[2,32,256,64]{2,0,1,3:T(2,128)} copy(f32[2,32,256,64]{3,2,1,0:T(8,128)} %bitcast.250) | data formatting | bytes 8388608 | tf_op jit(solution)/shard_map/all_to_all | solution.py:129
  544.6 11.5 %broadcast_select_fusion.1 = (f32[2,32,256,64]{2,0,1,3:T(2,128)S(1)}, f32[2,32,256,64]{2,0,1,3:T(2,128)}) fusion(f32[2,32,256,64]{2,0,1,3:T(2,128)} %copy.466, pred[64]{0:T(512)(128)(4,1)S(1)} %get-tuple-element.47, f32[2,32,256]{2,0,1:T(2,128)S(1)} %copy.464, f32[2,32,256,64]{2,0,1,3:T(2,128)} %copy.490, f32[2,32,256]{2,0,1:T(2,128)S(1)} %copy.488), kind=kLoop, calls=%fused_computation.22 | loop fusion | flops 2097152 | bytes 16908352 | tf_op jit(solution)/shard_map/jit(_where)/select_n | solution.py:142
  556.1 10.6 %fusion.18 = f32[2,1,32,256,64]{3,4,2,0,1:T(8,128)S(1)} fusion(f32[2,32,256,64]{2,0,1,3:T(2,128)} %get-tuple-element.44), kind=kOutput, calls=%fused_computation.34 | convolution fusion | flops 3222142976 | bytes 8388608 | tf_op jit(solution)/shard_map/abcde,dz->abcze/dot_general | solution.py:40
  566.8 6.4 fusion.15
  573.2 8.2 %fusion.12 = f32[2,1,32,256,64]{3,4,2,0,1:T(8,128)} fusion(f32[2,32,256,64]{2,0,1,3:T(2,128)S(1)} %get-tuple-element.43), kind=kOutput, calls=%fused_computation.32 | convolution fusion | flops 3222142976 | bytes 8388608 | tf_op jit(solution)/shard_map/abcde,dz->abcze/dot_general | solution.py:40
  581.4 8.4 %fusion.9 = f32[2,1,32,256,64]{3,4,2,0,1:T(8,128)} fusion(f32[2,32,256,64]{2,0,1,3:T(2,128)S(1)} %get-tuple-element.43), kind=kOutput, calls=%fused_computation.31 | convolution fusion | flops 3222142976 | bytes 8388608 | tf_op jit(solution)/shard_map/abcde,dz->abcze/dot_general | solution.py:40
  593.4 9.2 %copy.495 = f32[2,1,32,256,64]{4,2,0,1,3:T(8,128)} copy(f32[2,1,32,256,64]{3,4,2,0,1:T(8,128)} %pad_maximum_fusion.6) | data formatting | bytes 8388608 | tf_op jit(solution)/shard_map/stack | solution.py:53
  602.6 8.7 %reshape.453 = f32[2,1,524288]{2,1,0:T(1,128)} reshape(f32[256,1,2,32,64]{4,3,2,1,0:T(8,128)} %bitcast.260) | data formatting | bytes 8388608
  611.3 12.2 %all_to_all.109 = f32[2,1,524288]{2,1,0:T(1,128)} all-to-all(f32[2,1,524288]{2,1,0:T(1,128)} %reshape.453), channel_id=1, replica_groups=mesh['chain'=2,'px'=8,'py'=2] {'py'}, dimensions={0} | all-to-all | bytes 8388608 | tf_op jit(solution)/shard_map/all_to_all | solution.py:144
  623.5 16.5 %reduce.9 = f32[2,524288]{1,0:T(2,128)} reduce(f32[2,1,524288]{2,1,0:T(1,128)} %all_to_all.109, f32[]{:T(128)} %broadcast.356), dimensions={1}, to_apply=%all_to_all.99.reduce_sub_computation | reduce | bytes 8388612 | tf_op jit(solution)/shard_map/all_to_all | solution.py:144
  640.0 10.0 %reshape.454 = f32[256,1,2,32,64]{4,3,2,1,0:T(8,128)} reshape(f32[2,524288]{1,0:T(2,128)} %reduce.9) | data formatting | bytes 8388608
  650.0 12.2 %copy.496 = f32[2,1,32,256,64]{3,1,4,2,0:T(1,128)} copy(f32[2,1,32,256,64]{4,2,0,1,3:T(8,128)} %bitcast.261) | data formatting | bytes 8388608 | tf_op jit(solution)/shard_map/all_to_all | solution.py:144
  665.6 5.2 fusion.61
  674.4 9.2 %copy.471 = f32[2,1,32,256,64]{4,2,0,1,3:T(8,128)} copy(f32[2,1,32,256,64]{3,4,2,0,1:T(8,128)} %pad_maximum_fusion.4) | data formatting | bytes 8388608 | tf_op jit(solution)/shard_map/stack | solution.py:53
  683.6 8.7 %reshape.457 = f32[2,1,524288]{2,1,0:T(1,128)} reshape(f32[256,1,2,32,64]{4,3,2,1,0:T(8,128)} %bitcast.262) | data formatting | bytes 8388608
  692.3 11.8 %all_to_all.110 = f32[2,1,524288]{2,1,0:T(1,128)} all-to-all(f32[2,1,524288]{2,1,0:T(1,128)} %reshape.457), channel_id=1, replica_groups=mesh['chain'=2,'px'=8,'py'=2] {'py'}, dimensions={0} | all-to-all | bytes 8388608 | tf_op jit(solution)/shard_map/all_to_all | solution.py:144
  704.2 16.4 %reduce.10 = f32[2,524288]{1,0:T(2,128)} reduce(f32[2,1,524288]{2,1,0:T(1,128)} %all_to_all.110, f32[]{:T(128)} %broadcast.356), dimensions={1}, to_apply=%all_to_all.91.reduce_sub_computation | reduce | bytes 8388612 | tf_op jit(solution)/shard_map/all_to_all | solution.py:144
  720.6 10.0 %reshape.458 = f32[256,1,2,32,64]{4,3,2,1,0:T(8,128)} reshape(f32[2,524288]{1,0:T(2,128)} %reduce.10) | data formatting | bytes 8388608
  730.6 12.6 %copy.472 = f32[2,1,32,256,64]{3,1,4,2,0:T(1,128)} copy(f32[2,1,32,256,64]{4,2,0,1,3:T(8,128)} %bitcast.263) | data formatting | bytes 8388608 | tf_op jit(solution)/shard_map/all_to_all | solution.py:144
  746.0 3.6 fusion.63
  753.9 33.7 %multiply_add_fusion = f32[32,128,256]{2,1,0:T(8,128)} fusion(f32[32,128,256]{2,1,0:T(8,128)S(1)} %copy-done.11, f32[32,128,256]{2,1,0:T(8,128)S(1)} %copy-done.13, f32[32,128,256]{2,1,0:T(8,128)S(1)} %fusion.63, f32[32,128,256]{2,1,0:T(8,128)S(1)} %fusion.66, f32[32,128,128]{1,2,0:T(8,128)S(1)} %bitcast.284, f32[]{:T(128)} %bitcast.71, f32[]{:T(128)} %bitcast, ...), kind=kOutput, calls=%fused_computation.17 | convolution fusion | flops 1622212608 | bytes 23201288 | tf_op jit(solution)/shard_map/abcd,dz->abcz/dot_general | solution.py:40
  (124 shorter events, 70.8 us)
Async XLA Ops:
  0.0 8.3 %copy-start.8 = (f32[32,128,256]{2,1,0:T(8,128)S(1)}, f32[32,128,256]{2,1,0:T(8,128)}, u32[]{:S(2)}) copy-start(f32[32,128,256]{2,1,0:T(8,128)} %param.5) | copy-start | bytes 12582916
  1.0 7.2 copy-start.14
  1.0 7.2 copy-start.20
  1.0 7.2 copy-start.18
  2.0 6.3 copy-start.16
  34.8 8.5 %copy-start.2 = (f32[2,32,256,64]{2,3,1,0:T(8,128)S(1)}, f32[2,32,256,64]{2,3,1,0:T(8,128)}, u32[]{:S(2)}) copy-start(f32[2,32,256,64]{2,3,1,0:T(8,128)} %all_to_all.81) | copy-start | bytes 12582916
  57.3 3.6 copy-start.12
  59.5 1.3 copy-start.7
  88.5 101.1 %all-to-all-start.1 = ((f32[8,1,131072]{2,1,0:T(1,128)}), f32[8,1,131072]{2,1,0:T(1,128)}, u32[]{:S(2)}, u32[]{:S(2)}) async-start(f32[8,1,131072]{2,1,0:T(1,128)} %reshape.449), calls=%async_computation.1 | async-start | bytes 8388608 | tf_op jit(solution)/shard_map/all_to_all | solution.py:90
  233.9 7.8 copy-start.5
  247.3 1.3 copy-start.6
  286.4 97.3 %all-to-all-start.2 = ((f32[8,1,131072]{2,1,0:T(1,128)}), f32[8,1,131072]{2,1,0:T(1,128)}, u32[]{:S(2)}, u32[]{:S(2)}) async-start(f32[8,1,131072]{2,1,0:T(1,128)} %reshape.455), calls=%async_computation.2 | async-start | bytes 8388608 | tf_op jit(solution)/shard_map/all_to_all | solution.py:129
  291.0 7.7 copy-start.4
  326.0 62.4 %copy-start.22 = (s32[8]{0:T(128)S(1)}, s32[8]{0:T(128)}, u32[]{:S(2)}) copy-start(s32[8]{0:T(128)} %param.8) | copy-start | bytes 100
  326.0 62.5 %copy-start.23 = (s32[2]{0:T(128)S(1)}, s32[2]{0:T(128)}, u32[]{:S(2)}) copy-start(s32[2]{0:T(128)} %param.9) | copy-start | bytes 28
  383.7 97.3 %all-to-all-start.4 = ((f32[8,1,131072]{2,1,0:T(1,128)}), f32[8,1,131072]{2,1,0:T(1,128)}, u32[]{:S(2)}, u32[]{:S(2)}) async-start(f32[8,1,131072]{2,1,0:T(1,128)} %reshape.451), calls=%async_computation.4 | async-start | bytes 8388608 | tf_op jit(solution)/shard_map/all_to_all | solution.py:129
  417.5 3.3 copy-start
  509.4 5.7 copy-start.1
  556.1 10.7 %copy-start.3 = (f32[2,32,256,64]{2,0,1,3:T(2,128)S(1)}, f32[2,32,256,64]{2,0,1,3:T(2,128)}, u32[]{:S(2)}) copy-start(f32[2,32,256,64]{2,0,1,3:T(2,128)} %get-tuple-element.44) | copy-start | bytes 12582916
  664.7 1.0 copy-start.17
  664.7 0.9 copy-start.19
  664.7 6.1 copy-start.10
  665.0 5.9 copy-start.9
  746.0 4.0 copy-start.15
  746.0 4.0 copy-start.21
  750.0 3.9 copy-start.11
  750.0 3.9 copy-start.13
where the time goes:
time: 799 us; the launch traced here: 788 us
  local copies, waits for them, and re-layouts  290 us (36%)
  waiting for transfers between devices  172 us (22%)
  other arithmetic  139 us (17%)
  matrix products  138 us (17%)
  blocking collectives  31.6 us (4%)
  starting transfers between devices  16.9 us (2%)
    unnamed x71, local copies, waits for them, and re-layouts  128 us
    all_to_all x2, waiting for transfers between devices, on_device(): lax.all_to_all(product, 'px', split_axis=2, concat_axis=3, tiled=True)  116 us
    dot_general x12, matrix products, along(): jnp.einsum(letters + ',' + letters[axis] + 'z->' + result, field, table,...  104 us
    all_to_all x1, waiting for transfers between devices, on_device(): lax.all_to_all(columns, 'px', split_axis=2, concat_axis=1, tiled=True)  56.1 us
    another operation x4, local copies, waits for them, and re-layouts, rotate(): return jnp.stack([with_cos[0] - with_sin[1], with_cos[1] + with_sin[0]])  36.8 us
    unnamed x6, matrix products  34 us
    all_to_all x2, other arithmetic, on_device(): back = lax.all_to_all(back, 'py', split_axis=3, concat_axis=4, tiled=True)  32.9 us
    all_to_all x6, local copies, waits for them, and re-layouts, on_device(): lax.all_to_all(product, 'px', split_axis=2, concat_axis=3, tiled=True)  28.9 us
  transfers between devices with their start and end apart: 3, of which 3 were waited for; matrix products, arithmetic and copies ran while one was open for 13% of the time, Pallas kernels for 0%

commit v1 on v0

v1 whole, which is shorter than its diff:
```python
import functools
import math

import jax
import jax.numpy as jnp
import numpy as np
from jax import lax
from jax.experimental import pallas as pl
from jax.experimental.pallas import tpu as pltpu
from jax.sharding import PartitionSpec as P


def hartley(length):
    counter = np.arange(length, dtype=np.int64)
    angle = (counter[:, None] * counter[None, :] % length) * (2.0 * np.pi / length)
    return np.cos(angle) + np.sin(angle)


def chosen_index(freq_index, picked):
    ids = jnp.arange(freq_index.shape[0], dtype=jnp.int32)
    return jnp.sum(jnp.where(ids[None, :] == picked[:, None], freq_index[None, :], 0), axis=1)


def along(equation, field, table):
    return jnp.einsum(equation, field, jnp.asarray(table, jnp.float32), precision=lax.Precision.HIGH)


def plain_path(adjoint, saved, spectra, chosen):
    size_px, size_py = lax.axis_size("px"), lax.axis_size("py")
    one, two, three = adjoint.shape[0] * size_px, adjoint.shape[1] * size_py, adjoint.shape[2]
    t_one, t_two, t_three = hartley(one), hartley(two), hartley(three)
    width = three // size_py
    field = along("abc,cz->abz", adjoint, t_three)
    field = lax.all_to_all(field, "py", split_axis=2, concat_axis=1, tiled=True)
    field = along("abc,bz->azc", field, t_two)
    field = lax.all_to_all(field, "px", split_axis=1, concat_axis=0, tiled=True)
    spectrum = along("abc,az->zbc", field, t_one)
    kernels = lax.dynamic_slice_in_dim(spectra, lax.axis_index("py") * width, width, 3)
    omegas = chosen.astype(jnp.float32) * (math.pi / 8.0)
    scale = 1.0 / (one * two * three)
    total = jnp.zeros(saved.shape, jnp.float32)
    for slot in range(chosen.shape[0]):
        back = along("abc,az->zbc", spectrum * kernels[slot].astype(jnp.float32), t_one)
        back = lax.all_to_all(back, "px", split_axis=0, concat_axis=1, tiled=True)
        back = along("abc,bz->azc", back, t_two)
        back = lax.all_to_all(back, "py", split_axis=1, concat_axis=2, tiled=True)
        back = along("abc,cz->abz", back, t_three) * scale
        total = total + omegas[slot] * jnp.cos(omegas[slot] * saved) * back
    return total


def on_device(adjoint, saved, spectra, freq_index, picked):
    return plain_path(adjoint, saved, spectra, chosen_index(freq_index, picked))


def solution(mesh):
    placed = (
        P(("chain", "px"), "py", None),
        P(("chain", "px"), "py", None),
        P(None, None, "px", None),
        P(),
        P(),
    )
    return jax.shard_map(
        on_device,
        mesh=mesh,
        in_specs=placed,
        out_specs=P(("chain", "px"), "py", None),
        check_vma=False,
    )
```

time: 799 us -> 461 us (0.58)
  local copies, waits for them, and re-layouts: 290 us -> 81.2 us
  other arithmetic: 139 us -> 0.19 us
  waiting for transfers between devices: 172 us -> 251 us
  matrix products: 138 us -> 74.3 us
    unnamed x71 -> x18, local copies, waits for them, and re-layouts: 128 us -> 2.5 us
    all_to_all x3, waiting for transfers between devices: 172 us -> 251 us  [the longest x2 163 us: plain_path(): back = lax.all_to_all(back, 'px', split_axis=0, concat_axis=1, tiled=True)]
    all_to_all x5 -> x0, other arithmetic: 74.6 us -> none  [the longest x2 32.9 us: on_device(): back = lax.all_to_all(back, 'py', split_axis=3, concat_axis=4, tiled=True)]
    all_to_all x13 -> x8, local copies, waits for them, and re-layouts: 86.8 us -> 41 us  [the longest x4 25.5 us: plain_path(): back = lax.all_to_all(back, 'py', split_axis=1, concat_axis=2, tiled=True)]
    another operation x5 -> x0, local copies, waits for them, and re-layouts: 39.2 us -> none  [the longest x4 36.8 us: rotate(): return jnp.stack([with_cos[0] - with_sin[1], with_cos[1] + with_sin[0]])]
    unnamed x6 -> x0, matrix products: 34 us -> none
    dot_general x12 -> x9, matrix products: 104 us -> 74.3 us  [along(): jnp.einsum(equation, field, jnp.asarray(table, jnp.float32), precision=la...]
    select_n x6 -> x0, other arithmetic: 22.1 us -> none  [the longest x1 11.5 us: on_device(): jnp.where(first_slot, jnp.stack([untangled_real, untangled_imag])[..., No...]
  transfers between devices with their start and end apart: 3 -> 3, of which waited for: 3 -> 3; matrix products, arithmetic and copies ran while one was open for 13% -> 5% of each run, Pallas kernels for 0% -> 0%
where the time goes in v1:
time: 461 us; the launch traced here: 453 us
  waiting for transfers between devices  251 us (54%)
  local copies, waits for them, and re-layouts  81.2 us (18%)
  matrix products  74.3 us (16%)
  blocking collectives  28.8 us (6%)
  starting transfers between devices  17.2 us (4%)
    all_to_all x2, waiting for transfers between devices, plain_path(): back = lax.all_to_all(back, 'px', split_axis=0, concat_axis=1, tiled=True)  163 us
    all_to_all x1, waiting for transfers between devices, plain_path(): field = lax.all_to_all(field, 'px', split_axis=1, concat_axis=0, tiled=True)  88.8 us
    dot_general x9, matrix products, along(): jnp.einsum(equation, field, jnp.asarray(table, jnp.float32), precision=la...  74.3 us
    all_to_all x4, local copies, waits for them, and re-layouts, plain_path(): back = lax.all_to_all(back, 'py', split_axis=1, concat_axis=2, tiled=True)  25.5 us
    all_to_all x2, blocking collectives, plain_path(): back = lax.all_to_all(back, 'py', split_axis=1, concat_axis=2, tiled=True)  20.6 us
    transpose x3, local copies, waits for them, and re-layouts, along(): jnp.einsum(equation, field, jnp.asarray(table, jnp.float32), precision=la...  16.5 us
    dot_general x4, local copies, waits for them, and re-layouts, along(): jnp.einsum(equation, field, jnp.asarray(table, jnp.float32), precision=la...  16.2 us
    all_to_all x2, starting transfers between devices, plain_path(): back = lax.all_to_all(back, 'px', split_axis=0, concat_axis=1, tiled=True)  9.44 us
  transfers between devices with their start and end apart: 3, of which 3 were waited for; matrix products, arithmetic and copies ran while one was open for 5% of the time, Pallas kernels for 0%

profile of v1, /device:TPU:0, one launch (start us, length us, event | category | flops | bytes accessed | tf_op | source)
XLA Modules:
  0.0 453.3 jit_solution(6526546276658366027)
XLA Ops:
  0.0 3.7 convolution_bitcast_fusion.3
  3.7 2.4 copy.79
  6.1 8.2 %all_to_all.108 = f32[32,128,256]{1,0,2:T(8,128)} all-to-all(f32[32,128,256]{1,0,2:T(8,128)S(1)} %copy.79), channel_id=1, replica_groups=mesh['chain'=2,'px'=8,'py'=2] {'py'}, dimensions={2} | all-to-all | bytes 8388608 | tf_op jit(solution)/shard_map/all_to_all | solution.py:34
  14.3 5.2 %copy.80 = f32[32,128,256]{2,1,0:T(8,128)} copy(f32[32,128,256]{1,0,2:T(8,128)} %all_to_all.108) | data formatting | bytes 8388608 | tf_op jit(solution)/shard_map/all_to_all | solution.py:34
  19.5 0.0 copy-start.6
  19.5 4.8 %reshape.6 = f32[32,256,128]{2,1,0:T(8,128)} reshape(f32[32,128,256]{2,1,0:T(8,128)} %copy.80) | data formatting | bytes 8388608 | tf_op jit(solution)/shard_map/abc,bz->azc/dot_general | solution.py:25
  24.3 0.0 copy-done.6
  24.3 7.6 %convolution_bitcast_fusion.2 = f32[32,256,128]{1,2,0:T(8,128)} fusion(f32[32,256,128]{2,1,0:T(8,128)} %reshape.6, f32[256,256,1]{1,0,2:T(8,128)S(1)} %copy-done.6), kind=kOutput, calls=%fused_computation.11 | convolution fusion | flops 1610612736 | bytes 8650752 | tf_op jit(solution)/shard_map/abc,bz->azc/dot_general | solution.py:25
  31.9 5.5 %copy.82 = f32[32,256,128]{2,0,1:T(8,128)} copy(f32[32,256,128]{1,2,0:T(8,128)} %convolution_bitcast_fusion.2) | data formatting | bytes 8388608 | tf_op jit(solution)/shard_map/abc,bz->azc/transpose | solution.py:25
  37.5 7.7 %all-to-all-start.1 = ((f32[32,256,128]{2,0,1:T(8,128)}), f32[32,256,128]{2,0,1:T(8,128)}, u32[]{:S(2)}, u32[]{:S(2)}) async-start(f32[32,256,128]{2,0,1:T(8,128)} %copy.82), calls=%async_computation.1 | async-start | bytes 8388608 | tf_op jit(solution)/shard_map/all_to_all | solution.py:36
  45.2 4.3 constant_dynamic-slice_fusion.1
  49.5 0.0 copy-start.5
  49.5 88.8 %all-to-all-done.1 = f32[32,256,128]{2,0,1:T(8,128)} async-done(((f32[32,256,128]{2,0,1:T(8,128)}), f32[32,256,128]{2,0,1:T(8,128)}, u32[]{:S(2)}, u32[]{:S(2)}) %all-to-all-start.1) | async-done | bytes 4194336 | tf_op jit(solution)/shard_map/all_to_all | solution.py:36
  138.3 4.6 %copy.83 = f32[32,256,128]{2,1,0:T(8,128)S(1)} copy(f32[32,256,128]{2,0,1:T(8,128)} %all-to-all-done.1) | data formatting | bytes 8388608 | tf_op jit(solution)/shard_map/all_to_all | solution.py:36
  143.0 0.0 copy-done.5
  143.0 0.0 copy-start.2
  143.0 0.0 copy-start.3
  143.0 4.3 fusion.2
  147.3 0.0 copy-start
  147.3 2.0 copy-done
  149.3 0.0 copy-done.2
  149.3 0.0 copy-done.3
  149.3 2.7 fusion
  152.0 4.6 %copy.93 = f32[256,32,128]{2,1,0:T(8,128)} copy(f32[256,32,128]{2,0,1:T(8,128)S(1)} %fusion) | data formatting | bytes 8388608 | tf_op jit(solution)/shard_map/abc,az->zbc/dot_general | solution.py:25
  156.6 4.5 %all-to-all-start.4 = ((f32[256,32,128]{2,1,0:T(8,128)}), f32[256,32,128]{2,1,0:T(8,128)}, u32[]{:S(2)}, u32[]{:S(2)}) async-start(f32[256,32,128]{2,1,0:T(8,128)} %copy.93), calls=%async_computation.4 | async-start | bytes 8388608 | tf_op jit(solution)/shard_map/all_to_all | solution.py:44
  161.2 4.7 %fusion.1 = f32[256,32,128]{2,0,1:T(8,128)S(1)} fusion(f32[256,256,1]{0,1,2:T(8,128)S(1)} %copy-done.2, f32[256,32,128]{2,0,1:T(8,128)} %copy-done, bf16[1,256,32,128]{3,2,1,0:T(8,128)(2,1)S(1)} %get-tuple-element.6), kind=kOutput, calls=%fused_computation.3 | convolution fusion | flops 1612709888 | bytes 10747904 | tf_op jit(solution)/shard_map/abc,az->zbc/dot_general | solution.py:25
  165.9 4.4 copy.86
  170.3 83.5 %all-to-all-done.4 = f32[256,32,128]{2,1,0:T(8,128)} async-done(((f32[256,32,128]{2,1,0:T(8,128)}), f32[256,32,128]{2,1,0:T(8,128)}, u32[]{:S(2)}, u32[]{:S(2)}) %all-to-all-start.4) | async-done | bytes 4194336 | tf_op jit(solution)/shard_map/all_to_all | solution.py:44
  253.8 2.8 copy.94
  256.7 5.4 %convolution_bitcast_fusion = f32[32,256,128]{1,2,0:T(8,128)} fusion(f32[32,256,128]{2,1,0:T(8,128)S(1)} %bitcast.63, f32[256,256,1]{0,1,2:T(8,128)S(1)} %copy-done.2), kind=kOutput, calls=%fused_computation.9 | convolution fusion | flops 1610612736 | bytes 8650752 | tf_op jit(solution)/shard_map/abc,bz->azc/dot_general | solution.py:25
  262.1 5.5 %copy.97 = f32[32,256,128]{2,0,1:T(8,128)} copy(f32[32,256,128]{1,2,0:T(8,128)} %convolution_bitcast_fusion) | data formatting | bytes 8388608 | tf_op jit(solution)/shard_map/abc,bz->azc/transpose | solution.py:25
  267.5 11.9 %all_to_all.109 = f32[32,256,128]{2,0,1:T(8,128)} all-to-all(f32[32,256,128]{2,0,1:T(8,128)} %copy.97), channel_id=1, replica_groups=mesh['chain'=2,'px'=8,'py'=2] {'py'}, dimensions={1} | all-to-all | bytes 8388608 | tf_op jit(solution)/shard_map/all_to_all | solution.py:46
  279.5 0.0 copy-start.7
  279.5 0.0 copy-start.8
  279.5 4.9 %all-to-all-start.2 = ((f32[256,32,128]{2,1,0:T(8,128)}), f32[256,32,128]{2,1,0:T(8,128)}, u32[]{:S(2)}, u32[]{:S(2)}) async-start(f32[256,32,128]{2,1,0:T(8,128)} %copy.86), calls=%async_computation.2 | async-start | bytes 8388608 | tf_op jit(solution)/shard_map/all_to_all | solution.py:44
  284.4 0.0 copy-done.7
  284.4 0.0 copy-done.8
  284.4 0.2 fusion.4
  284.6 0.7 fusion.5
  285.3 7.4 %copy.126 = f32[32,2,128,128]{3,1,2,0:T(2,128)} copy(f32[32,2,128,128]{3,0,2,1:T(8,128)} %bitcast.61) | data formatting | bytes 8388608 | tf_op jit(solution)/shard_map/all_to_all | solution.py:46
  292.6 6.5 %all_to_all.101 = f32[32,128,256]{2,1,0:T(8,128)} reshape(f32[32,128,2,128]{3,2,1,0:T(2,128)} %bitcast.64) | data formatting | bytes 8388608 | tf_op jit(solution)/shard_map/all_to_all | solution.py:46
  299.1 79.0 %all-to-all-done.2 = f32[256,32,128]{2,1,0:T(8,128)} async-done(((f32[256,32,128]{2,1,0:T(8,128)}), f32[256,32,128]{2,1,0:T(8,128)}, u32[]{:S(2)}, u32[]{:S(2)}) %all-to-all-start.2) | async-done | bytes 4194336 | tf_op jit(solution)/shard_map/all_to_all | solution.py:44
  378.1 2.8 copy.87
  380.9 5.5 %convolution_bitcast_fusion.1 = f32[32,256,128]{1,2,0:T(8,128)} fusion(f32[32,256,128]{2,1,0:T(8,128)S(1)} %bitcast.65, f32[256,256,1]{0,1,2:T(8,128)S(1)} %copy-done.2), kind=kOutput, calls=%fused_computation.10 | convolution fusion | flops 1610612736 | bytes 8650752 | tf_op jit(solution)/shard_map/abc,bz->azc/dot_general | solution.py:25
  386.4 5.5 %copy.90 = f32[32,256,128]{2,0,1:T(8,128)} copy(f32[32,256,128]{1,2,0:T(8,128)} %convolution_bitcast_fusion.1) | data formatting | bytes 8388608 | tf_op jit(solution)/shard_map/abc,bz->azc/transpose | solution.py:25
  391.9 8.7 %all_to_all.110 = f32[32,256,128]{2,0,1:T(8,128)S(1)} all-to-all(f32[32,256,128]{2,0,1:T(8,128)} %copy.90), channel_id=1, replica_groups=mesh['chain'=2,'px'=8,'py'=2] {'py'}, dimensions={1} | all-to-all | bytes 8388608 | tf_op jit(solution)/shard_map/all_to_all | solution.py:46
  400.6 5.2 %copy.127 = f32[32,2,128,128]{3,1,2,0:T(2,128)} copy(f32[32,2,128,128]{3,0,2,1:T(8,128)S(1)} %bitcast.66) | data formatting | bytes 8388608 | tf_op jit(solution)/shard_map/all_to_all | solution.py:46
  405.8 6.4 %all_to_all.93 = f32[32,128,256]{2,1,0:T(8,128)} reshape(f32[32,128,2,128]{3,2,1,0:T(2,128)} %bitcast.67) | data formatting | bytes 8388608 | tf_op jit(solution)/shard_map/all_to_all | solution.py:46
  412.3 0.0 copy-start.1
  412.3 0.0 copy-start.4
  412.3 4.2 fusion.6
  416.5 0.0 copy-done.1
  416.5 0.5 copy-done.4
  417.0 36.1 %multiply_add_fusion = f32[32,128,256]{2,1,0:T(8,128)} fusion(f32[32,128,256]{2,1,0:T(8,128)S(1)} %copy-done.4, f32[32,128,256]{2,1,0:T(8,128)S(1)} %fusion.6, f32[32,128,256]{2,1,0:T(8,128)S(1)} %copy-done.1, f32[256,256,1]{0,1,2:T(8,128)S(1)} %copy-done.2, f32[]{:T(128)} %bitcast.16, f32[]{:T(128)} %bitcast), kind=kOutput, calls=%fused_computation.8 | convolution fusion | flops 1620049920 | bytes 17039368 | tf_op jit(solution)/shard_map/abc,cz->abz/dot_general | solution.py:25
  (1 shorter events, 0.0 us)
Async XLA Ops:
  19.5 4.8 %copy-start.6 = (f32[256,256,1]{1,0,2:T(8,128)S(1)}, f32[256,256,1]{1,0,2:T(8,128)}, u32[]{:S(2)}) copy-start(f32[256,256,1]{1,0,2:T(8,128)} %constant.25) | copy-start | bytes 786436
  37.5 100.9 %all-to-all-start.1 = ((f32[32,256,128]{2,0,1:T(8,128)}), f32[32,256,128]{2,0,1:T(8,128)}, u32[]{:S(2)}, u32[]{:S(2)}) async-start(f32[32,256,128]{2,0,1:T(8,128)} %copy.82), calls=%async_computation.1 | async-start | bytes 8388608 | tf_op jit(solution)/shard_map/all_to_all | solution.py:36
  49.5 93.4 %copy-start.5 = (f32[256,256,1]{0,1,2:T(8,128)S(1)}, f32[256,256,1]{0,1,2:T(8,128)}, u32[]{:S(2)}) copy-start(f32[256,256,1]{0,1,2:T(8,128)} %constant.24) | copy-start | bytes 786436
  143.0 6.3 %copy-start.2 = (f32[256,256,1]{0,1,2:T(8,128)S(1)}, f32[256,256,1]{0,1,2:T(8,128)}, u32[]{:S(2)}) copy-start(f32[256,256,1]{0,1,2:T(8,128)} %constant.23) | copy-start | bytes 786436
  143.0 6.3 %copy-start.3 = (bf16[1,256,32,128]{3,2,1,0:T(8,128)(2,1)S(1)}, bf16[1,256,32,128]{3,2,1,0:T(8,128)(2,1)}, u32[]{:S(2)}) copy-start(bf16[1,256,32,128]{3,2,1,0:T(8,128)(2,1)} %get-tuple-element.5) | copy-start | bytes 6291460
  147.3 2.0 copy-start
  156.6 97.2 %all-to-all-start.4 = ((f32[256,32,128]{2,1,0:T(8,128)}), f32[256,32,128]{2,1,0:T(8,128)}, u32[]{:S(2)}, u32[]{:S(2)}) async-start(f32[256,32,128]{2,1,0:T(8,128)} %copy.93), calls=%async_computation.4 | async-start | bytes 8388608 | tf_op jit(solution)/shard_map/all_to_all | solution.py:44
  279.5 4.9 %copy-start.7 = (s32[8]{0:T(128)S(1)}, s32[8]{0:T(128)}, u32[]{:S(2)}) copy-start(s32[8]{0:T(128)} %param.17) | copy-start | bytes 100
  279.5 4.9 %copy-start.8 = (s32[2]{0:T(128)S(1)}, s32[2]{0:T(128)}, u32[]{:S(2)}) copy-start(s32[2]{0:T(128)} %param.18) | copy-start | bytes 28
  279.5 98.6 %all-to-all-start.2 = ((f32[256,32,128]{2,1,0:T(8,128)}), f32[256,32,128]{2,1,0:T(8,128)}, u32[]{:S(2)}, u32[]{:S(2)}) async-start(f32[256,32,128]{2,1,0:T(8,128)} %copy.86), calls=%async_computation.2 | async-start | bytes 8388608 | tf_op jit(solution)/shard_map/all_to_all | solution.py:44
  412.3 4.3 copy-start.1
  412.3 4.7 %copy-start.4 = (f32[32,128,256]{2,1,0:T(8,128)S(1)}, f32[32,128,256]{2,1,0:T(8,128)}, u32[]{:S(2)}) copy-start(f32[32,128,256]{2,1,0:T(8,128)} %param.15) | copy-start | bytes 12582916

commit v2 on v1

--- a/solution.py
+++ b/solution.py
@@ -49,8 +49,316 @@
     return total
 
 
+def as_three(matrix, axis):
+    high = matrix.astype(jnp.bfloat16)
+    low = (matrix - high.astype(np.float64)).astype(jnp.bfloat16)
+    order = (high, high, low)
+    return jnp.asarray(np.concatenate(order, axis=axis))
+
+
+def split(value, axis):
+    high = value.astype(jnp.bfloat16)
+    low = (value - high.astype(jnp.float32)).astype(jnp.bfloat16)
+    return jnp.concatenate([high, low, high], axis=axis)
+
+
+def from_right(rows, table):
+    return jnp.dot(split(rows, 1), table, preferred_element_type=jnp.float32)
+
+
+def from_left(table, columns):
+    return jnp.dot(table, split(columns, 0), preferred_element_type=jnp.float32)
+
+
+def params(**more):
+    return pltpu.CompilerParams(vmem_limit_bytes=58 << 20, **more)
+
+
+def third_kernel(field_ref, table_ref, out_ref):
+    planes, lines, three = field_ref.shape
+    parts, _, _, width = out_ref.shape
+    result = from_right(field_ref[...].reshape(planes * lines, three), table_ref[...])
+    for part in range(parts):
+        piece = result[:, part * width : (part + 1) * width]
+        out_ref[part] = piece.reshape(planes, lines, width)
+
+
+def second_kernel(field_ref, table_ref, out_ref, held):
+    parts, planes, _, width = field_ref.shape
+    size_px, local, _, _ = out_ref.shape
+    for plane in range(0, planes, 2):
+        sides = [
+            jnp.concatenate([field_ref[part, at] for part in range(parts)], axis=0)
+            for at in (plane, plane + 1)
+        ]
+        result = from_left(table_ref[...], jnp.concatenate(sides, axis=1))
+        held[plane] = result[:, :width]
+        held[plane + 1] = result[:, width:]
+    for peer in range(size_px):
+        out_ref[peer] = jnp.swapaxes(held[:, peer * local : (peer + 1) * local, :], 0, 1)
+
+
+def second_back_kernel(field_ref, table_ref, out_ref, held):
+    _, size_px, local, planes, width = field_ref.shape
+    parts, _, _, lines, _ = out_ref.shape
+    for peer in range(size_px):
+        held[:, peer * local : (peer + 1) * local, :] = jnp.swapaxes(field_ref[0, peer], 0, 1)
+    for plane in range(0, planes, 2):
+        columns = jnp.concatenate([held[plane], held[plane + 1]], axis=1)
+        result = from_left(table_ref[...], columns)
+        for part in range(parts):
+            rows = result[part * lines : (part + 1) * lines]
+            out_ref[part, 0, plane] = rows[:, :width]
+            out_ref[part, 0, plane + 1] = rows[:, width:]
+
+
+def cosine_turns(turns):
+    turns = turns - jnp.floor(turns + 0.5)
+    square = turns * turns * (4.0 * math.pi * math.pi)
+    value = jnp.full_like(square, 1.0 / math.factorial(20))
+    for order in range(9, -1, -1):
+        value = value * square + (-1.0) ** order / math.factorial(2 * order)
+    return value
+
+
+def third_back_kernel(scale, chosen_ref, field_ref, saved_ref, table_ref, out_ref):
+    parts, slots, planes, lines, width = field_ref.shape
+    three = parts * width
+    total = None
+    site = saved_ref[...].reshape(planes * lines, three)
+    for slot in range(slots):
+        sides = [field_ref[part, slot].reshape(planes * lines, width) for part in range(parts)]
+        field = from_right(jnp.concatenate(sides, axis=1), table_ref[...])
+        index = chosen_ref[slot].astype(jnp.float32)
+        weight = cosine_turns(site * (index * (1.0 / 16.0))) * (index * (math.pi / 8.0 * scale))
+        total = weight * field if total is None else total + weight * field
+    out_ref[...] = total.reshape(planes, lines, three)
+
+
+def middle_kernel(
+    chunks,
+    field_ref,
+    spectra_ref,
+    table_ref,
+    out_ref,
+    gathered,
+    raw,
+    kernels,
+    product,
+    go_send,
+    go_recv,
+    back_send,
+    back_recv,
+    own_sem,
+    back_own,
+    raw_sem,
+):
+    size_px, local, planes, width = field_ref.shape
+    slots, one = raw.shape[0], raw.shape[1]
+    step = local // chunks
+    me = lax.axis_index("px")
+    part = lax.axis_index("py")
+
+    def peer_of(turn):
+        return lax.rem(me + turn, size_px)
+
+    def go(chunk, sender, receiver):
+        rows = pl.ds(chunk * step, step)
+        return pltpu.make_async_remote_copy(
+            src_ref=field_ref.at[receiver, rows],
+            dst_ref=gathered.at[sender, rows],
+            send_sem=go_send.at[chunk, receiver],
+            recv_sem=go_recv.at[chunk, sender],
+            device_id={"px": receiver},
+            device_id_type=pl.DeviceIdType.MESH,
+        )
+
+    def back(slot, chunk, sender, receiver):
+        rows = pl.ds(chunk * step, step)
+        return pltpu.make_async_remote_copy(
+            src_ref=product.at[slot, receiver, rows],
+            dst_ref=out_ref.at[slot, sender, rows],
+            send_sem=back_send.at[slot, chunk, receiver],
+            recv_sem=back_recv.at[slot, chunk, sender],
+            device_id={"px": receiver},
+            device_id_type=pl.DeviceIdType.MESH,
+        )
+
+    own = pltpu.make_async_copy(field_ref.at[me], gathered.at[me], own_sem)
+    fetch = pltpu.make_async_copy(spectra_ref.at[:, :, :, pl.ds(part * width, width)], raw, raw_sem)
+    own.start()
+    fetch.start()
+
+    barrier = pltpu.get_barrier_semaphore()
+
+    @pl.loop(1, size_px)
+    def _(turn):
+        pl.semaphore_signal(
+            barrier, inc=1, device_id={"px": peer_of(turn)}, device_id_type=pl.DeviceIdType.MESH
+        )
+
+    pl.semaphore_wait(barrier, size_px - 1)
+
+    @pl.loop(0, chunks)
+    def _(chunk):
+        @pl.loop(1, size_px)
+        def _(turn):
+            go(chunk, me, peer_of(turn)).start()
+
+    own.wait()
+    fetch.wait()
+    block = 16
+
+    @pl.loop(0, one // block)
+    def _(at):
+        rows = pl.ds(pl.multiple_of(at * block, block), block)
+        for slot in range(slots):
+            piece = raw[slot, rows].astype(jnp.float32)
+            kernels[slot, :, rows, :] = jnp.swapaxes(piece, 0, 1)
+
+    @pl.loop(0, chunks)
+    def _(chunk):
+        @pl.loop(1, size_px)
+        def _(turn):
+            go(chunk, peer_of(turn), me).wait_recv()
+
+        @pl.loop(0, step // 2)
+        def _(pair):
+            first = chunk * step + pair * 2
+            second = first + 1
+            columns = jnp.concatenate(
+                [gathered[:, at].reshape(one, width) for at in (first, second)], axis=1
+            )
+            spectrum = from_left(table_ref[...], columns)
+            for slot in range(slots):
+                factor = jnp.concatenate([kernels[slot, first], kernels[slot, second]], axis=1)
+                result = from_left(table_ref[...], spectrum * factor)
+                product[slot, :, first] = result[:, :width].reshape(size_px, planes, width)
+                product[slot, :, second] = result[:, width:].reshape(size_px, planes, width)
+
+        for slot in range(slots):
+
+            @pl.loop(1, size_px)
+            def _(turn):
+                back(slot, chunk, me, peer_of(turn)).start()
+
+    homes = [
+        pltpu.make_async_copy(product.at[slot, me], out_ref.at[slot, me], back_own.at[slot])
+        for slot in range(slots)
+    ]
+    for home in homes:
+        home.start()
+
+    @pl.loop(0, chunks)
+    def _(chunk):
+        @pl.loop(1, size_px)
+        def _(turn):
+            peer = peer_of(turn)
+            go(chunk, me, peer).wait_send()
+            for slot in range(slots):
+                back(slot, chunk, me, peer).wait_send()
+                back(slot, chunk, peer, me).wait_recv()
+
+    for home in homes:
+        home.wait()
+
+
+def kernel_path(adjoint, saved, spectra, chosen):
+    size_px, size_py = lax.axis_size("px"), lax.axis_size("py")
+    planes, lines, three = adjoint.shape
+    one, two = planes * size_px, lines * size_py
+    width, local, slots = three // size_py, spectra.shape[2], chosen.shape[0]
+    whole = lambda table: pl.BlockSpec(table.shape, lambda *at: (0,) * table.ndim)
+    anywhere = pl.BlockSpec(memory_space=pl.ANY)
+    f32 = jnp.float32
+    block = 8
+    right_three = as_three(hartley(three), 0)
+    left_two, left_one = as_three(hartley(two), 1), as_three(hartley(one), 1)
+
+    field = pl.pallas_call(
+        third_kernel,
+        grid=(planes // block,),
+        in_specs=[pl.BlockSpec((block, lines, three), lambda i: (i, 0, 0)), whole(right_three)],
+        out_specs=pl.BlockSpec((size_py, block, lines, width), lambda i: (0, i, 0, 0)),
+        out_shape=jax.ShapeDtypeStruct((size_py, planes, lines, width), f32),
+        compiler_params=params(),
+        name="third",
+    )(adjoint, right_three)
+    field = lax.all_to_all(field, "py", split_axis=0, concat_axis=0, tiled=True)
+    field = pl.pallas_call(
+        second_kernel,
+        grid=(planes // block,),
+        in_specs=[
+            pl.BlockSpec((size_py, block, lines, width), lambda i: (0, i, 0, 0)),
+            whole(left_two),
+        ],
+        out_specs=pl.BlockSpec((size_px, local, block, width), lambda i: (0, 0, i, 0)),
+        out_shape=jax.ShapeDtypeStruct((size_px, local, planes, width), f32),
+        scratch_shapes=[pltpu.VMEM((block, two, width), f32)],
+        compiler_params=params(),
+        name="second",
+    )(field, left_two)
+    chunks = 4
+    dma = pltpu.SemaphoreType.DMA
+    field = pl.pallas_call(
+        functools.partial(middle_kernel, chunks),
+        in_specs=[anywhere, anywhere, pl.BlockSpec(memory_space=pltpu.VMEM)],
+        out_specs=anywhere,
+        out_shape=jax.ShapeDtypeStruct((slots, size_px, local, planes, width), f32),
+        scratch_shapes=[
+            pltpu.VMEM((size_px, local, planes, width), f32),
+            pltpu.VMEM((slots, one, local, width), spectra.dtype),
+            pltpu.VMEM((slots, local, one, width), f32),
+            pltpu.VMEM((slots, size_px, local, planes, width), f32),
+            dma((chunks, size_px)),
+            dma((chunks, size_px)),
+            dma((slots, chunks, size_px)),
+            dma((slots, chunks, size_px)),
+            dma,
+            dma((slots,)),
+            dma,
+        ],
+        compiler_params=params(collective_id=0, has_side_effects=True),
+        name="middle",
+    )(field, spectra, left_one)
+    field = pl.pallas_call(
+        second_back_kernel,
+        grid=(slots, planes // block),
+        in_specs=[
+            pl.BlockSpec((1, size_px, local, block, width), lambda j, i: (j, 0, 0, i, 0)),
+            whole(left_two),
+        ],
+        out_specs=pl.BlockSpec((size_py, 1, block, lines, width), lambda j, i: (0, j, i, 0, 0)),
+        out_shape=jax.ShapeDtypeStruct((size_py, slots, planes, lines, width), f32),
+        scratch_shapes=[pltpu.VMEM((block, two, width), f32)],
+        compiler_params=params(),
+        name="second_back",
+    )(field, left_two)
+    field = lax.all_to_all(field, "py", split_axis=0, concat_axis=0, tiled=True)
+    scale = 1.0 / (one * two * three)
+    piece = 4
+    return pl.pallas_call(
+        functools.partial(third_back_kernel, scale),
+        grid=(planes // piece,),
+        in_specs=[
+            pl.BlockSpec(memory_space=pltpu.SMEM),
+            pl.BlockSpec((size_py, slots, piece, lines, width), lambda i: (0, 0, i, 0, 0)),
+            pl.BlockSpec((piece, lines, three), lambda i: (i, 0, 0)),
+            whole(right_three),
+        ],
+        out_specs=pl.BlockSpec((piece, lines, three), lambda i: (i, 0, 0)),
+        out_shape=jax.ShapeDtypeStruct((planes, lines, three), f32),
+        compiler_params=params(),
+        name="third_back",
+    )(chosen, field, saved, right_three)
+
+
 def on_device(adjoint, saved, spectra, freq_index, picked):
-    return plain_path(adjoint, saved, spectra, chosen_index(freq_index, picked))
+    chosen = chosen_index(freq_index, picked)
+    width = adjoint.shape[2] // lax.axis_size("py")
+    if adjoint.shape[0] % 8 == 0 and spectra.shape[2] % 8 == 0 and width % 128 == 0:
+        return kernel_path(adjoint, saved, spectra, chosen)
+    return plain_path(adjoint, saved, spectra, chosen)
 
 
 def solution(mesh):

time: 461 us -> 342 us (0.74)
  the two profiles are of different devices: /device:TPU:0 before, /device:TPU:11 now
where the time goes in v2:
time: 342 us; the launch traced here: 341 us
  Pallas kernels  314 us (92%)
  blocking collectives  12.2 us (4%)
  starting transfers between devices  7.55 us (2%)
  waiting for transfers between devices  6.4 us (2%)
    pallas_call x1, Pallas kernels, kernel_path(): pl.pallas_call(functools.partial(middle_kernel, chunks), in_specs=[anywhe...  278 us
    pallas_call x1, Pallas kernels, kernel_path(): pl.pallas_call(functools.partial(third_back_kernel, scale), grid=(planes...  13.7 us
    all_to_all x1, blocking collectives, kernel_path(): field = lax.all_to_all(field, 'py', split_axis=0, concat_axis=0, tiled=True)  12.2 us
    pallas_call x1, Pallas kernels, kernel_path(): pl.pallas_call(second_back_kernel, grid=(slots, planes // block), in_spec...  10.7 us
    all_to_all x1, starting transfers between devices, kernel_path(): field = lax.all_to_all(field, 'py', split_axis=0, concat_axis=0, tiled=True)  7.55 us
  transfers between devices with their start and end apart: 1, of which 1 were waited for; matrix products, arithmetic and copies ran while one was open for 0% of the time, Pallas kernels for 0%

profile of v2, /device:TPU:11, one launch (start us, length us, event | category | flops | bytes accessed | tf_op | source)
XLA Modules:
  0.0 341.0 jit_solution(10108586809960529433)
XLA Ops:
  0.0 5.9 %third.1 = f32[2,32,128,128]{3,2,1,0:T(8,128)} custom-call(f32[32,128,256]{2,1,0:T(8,128)} %field_ref.1, bf16[768,256]{1,0:T(8,128)(2,1)} %constant.6.clone.table_ref), custom_call_target="tpu_custom_call" | custom-call | tf_op jit(solution)/shard_map/third/pallas_call | solution.py:278
  5.9 12.2 %all_to_all.10.field_ref = f32[2,32,128,128]{3,2,1,0:T(8,128)} all-to-all(f32[2,32,128,128]{3,2,1,0:T(8,128)} %third.1), channel_id=1, replica_groups=mesh['chain'=2,'px'=8,'py'=2] {'py'}, dimensions={0} | all-to-all | bytes 8388608 | tf_op jit(solution)/shard_map/all_to_all | solution.py:287
  18.1 5.9 %second.1.field_ref = f32[8,32,32,128]{3,2,1,0:T(8,128)} custom-call(f32[2,32,128,128]{3,2,1,0:T(8,128)} %all_to_all.10.field_ref, bf16[256,768]{1,0:T(8,128)(2,1)} %constant.7.clone.table_ref), custom_call_target="tpu_custom_call" | custom-call | tf_op jit(solution)/shard_map/second/pallas_call | solution.py:288
  24.0 277.8 %middle.1.field_ref = f32[2,8,32,32,128]{4,3,2,1,0:T(8,128)} custom-call(f32[8,32,32,128]{3,2,1,0:T(8,128)} %second.1.field_ref, bf16[2,256,32,256]{3,2,1,0:T(8,128)(2,1)} %spectra_ref.1, bf16[256,768]{1,0:T(8,128)(2,1)} %constant.7.clone.table_ref), custom_call_target="tpu_custom_call" | custom-call | tf_op jit(solution)/shard_map/middle/pallas_call | solution.py:303
  301.9 10.7 %second_back.1 = f32[2,2,32,128,128]{4,3,2,1,0:T(8,128)} custom-call(f32[2,8,32,32,128]{4,3,2,1,0:T(8,128)} %middle.1.field_ref, bf16[256,768]{1,0:T(8,128)(2,1)} %constant.7.clone.table_ref), custom_call_target="tpu_custom_call" | custom-call | tf_op jit(solution)/shard_map/second_back/pallas_call | solution.py:324
  312.6 0.0 copy-start
  312.6 0.0 copy-start.1
  312.6 7.6 %all-to-all-start.1 = ((f32[2,2,32,128,128]{4,3,2,1,0:T(8,128)}), f32[2,2,32,128,128]{4,3,2,1,0:T(8,128)}, u32[]{:S(2)}, u32[]{:S(2)}) async-start(f32[2,2,32,128,128]{4,3,2,1,0:T(8,128)} %second_back.1), calls=%async_computation.1 | async-start | bytes 16777216 | tf_op jit(solution)/shard_map/all_to_all | solution.py:337
  320.1 0.0 copy-done
  320.1 0.0 copy-done.1
  320.1 0.7 fusion.chosen_ref
  320.9 6.4 %all-to-all-done.1.field_ref = f32[2,2,32,128,128]{4,3,2,1,0:T(8,128)} async-done(((f32[2,2,32,128,128]{4,3,2,1,0:T(8,128)}), f32[2,2,32,128,128]{4,3,2,1,0:T(8,128)}, u32[]{:S(2)}, u32[]{:S(2)}) %all-to-all-start.1) | async-done | bytes 8388640 | tf_op jit(solution)/shard_map/all_to_all | solution.py:337
  327.3 13.7 %third_back.1 = f32[32,128,256]{2,1,0:T(8,128)} custom-call(s32[2]{0:T(128)} %fusion.chosen_ref, f32[2,2,32,128,128]{4,3,2,1,0:T(8,128)} %all-to-all-done.1.field_ref, f32[32,128,256]{2,1,0:T(8,128)} %saved_ref.1, bf16[768,256]{1,0:T(8,128)(2,1)} %constant.6.clone.table_ref), custom_call_target="tpu_custom_call" | custom-call | tf_op jit(solution)/shard_map/third_back/pallas_call | solution.py:340
Async XLA Ops:
  312.6 7.6 %copy-start = (s32[8]{0:T(128)S(1)}, s32[8]{0:T(128)}, u32[]{:S(2)}) copy-start(s32[8]{0:T(128)} %param.11) | copy-start | bytes 100
  312.6 7.6 %copy-start.1 = (s32[2]{0:T(128)S(1)}, s32[2]{0:T(128)}, u32[]{:S(2)}) copy-start(s32[2]{0:T(128)} %param.12) | copy-start | bytes 28
  312.6 14.7 %all-to-all-start.1 = ((f32[2,2,32,128,128]{4,3,2,1,0:T(8,128)}), f32[2,2,32,128,128]{4,3,2,1,0:T(8,128)}, u32[]{:S(2)}, u32[]{:S(2)}) async-start(f32[2,2,32,128,128]{4,3,2,1,0:T(8,128)} %second_back.1), calls=%async_computation.1 | async-start | bytes 16777216 | tf_op jit(solution)/shard_map/all_to_all | solution.py:337

commit v3 on v2

--- a/solution.py
+++ b/solution.py
@@ -149,42 +149,64 @@
     go_recv,
     back_send,
     back_recv,
+    plane_send,
+    plane_recv,
     own_sem,
     back_own,
     raw_sem,
 ):
-    size_px, local, planes, width = field_ref.shape
+    half, rows_all, planes, width = field_ref.shape
+    size_px, local = 2 * half, rows_all // 2
     slots, one = raw.shape[0], raw.shape[1]
     step = local // chunks
     me = lax.axis_index("px")
     part = lax.axis_index("py")
-
-    def peer_of(turn):
-        return lax.rem(me + turn, size_px)
+    lower = me < half
+    base = jnp.where(lower, 0, half)
+    place = me - base
+
+    def block_of(owner):
+        return jnp.where(owner < half, owner, size_px - 1 - owner)
+
+    def other(turn):
+        return half - base + lax.rem(place + turn, half)
+
+    def mate(turn):
+        return base + lax.rem(place + turn, half)
+
+    def to(index):
+        return dict(device_id={"px": index}, device_id_type=pl.DeviceIdType.MESH)
 
     def go(chunk, sender, receiver):
-        rows = pl.ds(chunk * step, step)
+        rows = pl.ds(chunk * 2 * step, 2 * step)
         return pltpu.make_async_remote_copy(
-            src_ref=field_ref.at[receiver, rows],
+            src_ref=field_ref.at[block_of(receiver), rows],
             dst_ref=gathered.at[sender, rows],
             send_sem=go_send.at[chunk, receiver],
             recv_sem=go_recv.at[chunk, sender],
-            device_id={"px": receiver},
-            device_id_type=pl.DeviceIdType.MESH,
+            **to(receiver),
         )
 
     def back(slot, chunk, sender, receiver):
-        rows = pl.ds(chunk * step, step)
+        rows = pl.ds(chunk * 2 * step, 2 * step)
         return pltpu.make_async_remote_copy(
-            src_ref=product.at[slot, receiver, rows],
-            dst_ref=out_ref.at[slot, sender, rows],
-            send_sem=back_send.at[slot, chunk, receiver],
-            recv_sem=back_recv.at[slot, chunk, sender],
-            device_id={"px": receiver},
-            device_id_type=pl.DeviceIdType.MESH,
+            src_ref=product.at[slot, receiver - base, rows],
+            dst_ref=out_ref.at[slot, block_of(sender), rows],
+            send_sem=back_send.at[slot, chunk, receiver - base],
+            recv_sem=back_recv.at[slot, chunk, sender - base],
+            **to(receiver),
         )
 
-    own = pltpu.make_async_copy(field_ref.at[me], gathered.at[me], own_sem)
+    def plane(kind, send, receiver):
+        return pltpu.make_async_remote_copy(
+            src_ref=kernels.at[:, 0],
+            dst_ref=kernels.at[:, local + kind],
+            send_sem=plane_send.at[send],
+            recv_sem=plane_recv.at[kind],
+            **to(receiver),
+        )
+
+    own = pltpu.make_async_copy(field_ref.at[block_of(me)], gathered.at[me], own_sem)
     fetch = pltpu.make_async_copy(spectra_ref.at[:, :, :, pl.ds(part * width, width)], raw, raw_sem)
     own.start()
     fetch.start()
@@ -193,18 +215,23 @@
 
     @pl.loop(1, size_px)
     def _(turn):
-        pl.semaphore_signal(
-            barrier, inc=1, device_id={"px": peer_of(turn)}, device_id_type=pl.DeviceIdType.MESH
-        )
+        pl.semaphore_signal(barrier, inc=1, **to(lax.rem(me + turn, size_px)))
 
     pl.semaphore_wait(barrier, size_px - 1)
 
-    @pl.loop(0, chunks)
-    def _(chunk):
-        @pl.loop(1, size_px)
-        def _(turn):
-            go(chunk, me, peer_of(turn)).start()
-
+    def send_chunk(at):
+        chunk = chunks - 1 - at
+
+        @pl.loop(0, half)
+        def _(turn):
+            go(chunk, me, other(turn)).start()
+
+        @pl.loop(1, half)
+        def _(turn):
+            go(chunk, me, mate(turn)).start()
+
+    early = chunks // 2
+    pl.loop(0, early)(send_chunk)
     own.wait()
     fetch.wait()
     block = 16
@@ -214,36 +241,73 @@
         rows = pl.ds(pl.multiple_of(at * block, block), block)
         for slot in range(slots):
             piece = raw[slot, rows].astype(jnp.float32)
-            kernels[slot, :, rows, :] = jnp.swapaxes(piece, 0, 1)
+            kernels[slot, 0:local, rows, :] = jnp.swapaxes(piece, 0, 1)
+
+    before = lax.rem(me + size_px - 1, size_px)
+    ends = (me == 0) | (me == size_px - 1)
+
+    @pl.when(before >= half)
+    def _():
+        plane(0, 0, before).start()
+
+    @pl.when(me == half)
+    def _():
+        plane(1, 1, 0).start()
+        plane(1, 2, size_px - 1).start()
+
+    pl.loop(early, chunks)(send_chunk)
 
     @pl.loop(0, chunks)
-    def _(chunk):
-        @pl.loop(1, size_px)
-        def _(turn):
-            go(chunk, peer_of(turn), me).wait_recv()
-
-        @pl.loop(0, step // 2)
-        def _(pair):
-            first = chunk * step + pair * 2
-            second = first + 1
+    def _(at):
+        chunk = chunks - 1 - at
+
+        @pl.loop(0, half)
+        def _(turn):
+            go(chunk, other(turn), me).wait_recv()
+
+        @pl.loop(1, half)
+        def _(turn):
+            go(chunk, mate(turn), me).wait_recv()
+
+        @pl.when(chunk == 0)
+        def _():
+            @pl.when(jnp.logical_not(lower))
+            def _():
+                plane(0, 0, before).wait_recv()
+
+            @pl.when(ends)
+            def _():
+                plane(1, 1, before).wait_recv()
+
+        own_sites = pl.ds(pl.multiple_of(base * planes, half * planes), half * planes)
+
+        @pl.loop(0, step)
+        def _(inner):
+            line = chunk * step + inner
+            first, second = 2 * line, 2 * line + 1
             columns = jnp.concatenate(
                 [gathered[:, at].reshape(one, width) for at in (first, second)], axis=1
             )
             spectrum = from_left(table_ref[...], columns)
+            leading = line == 0
+            plain = jnp.where(lower, line, local - line)
+            mirrored = jnp.where(leading & ends, local + 1, plain)
             for slot in range(slots):
-                factor = jnp.concatenate([kernels[slot, first], kernels[slot, second]], axis=1)
-                result = from_left(table_ref[...], spectrum * factor)
-                product[slot, :, first] = result[:, :width].reshape(size_px, planes, width)
-                product[slot, :, second] = result[:, width:].reshape(size_px, planes, width)
+                factor = jnp.concatenate([kernels[slot, plain], kernels[slot, mirrored]], axis=1)
+                result = from_left(table_ref[own_sites, :], spectrum * factor)
+                product[slot, :, first] = result[:, :width].reshape(half, planes, width)
+                product[slot, :, second] = result[:, width:].reshape(half, planes, width)
 
         for slot in range(slots):
 
-            @pl.loop(1, size_px)
+            @pl.loop(1, half)
             def _(turn):
-                back(slot, chunk, me, peer_of(turn)).start()
+                back(slot, chunk, me, mate(turn)).start()
 
     homes = [
-        pltpu.make_async_copy(product.at[slot, me], out_ref.at[slot, me], back_own.at[slot])
+        pltpu.make_async_copy(
+            product.at[slot, place], out_ref.at[slot, block_of(me)], back_own.at[slot]
+        )
         for slot in range(slots)
     ]
     for home in homes:
@@ -253,14 +317,31 @@
     def _(chunk):
         @pl.loop(1, size_px)
         def _(turn):
-            peer = peer_of(turn)
-            go(chunk, me, peer).wait_send()
+            go(chunk, me, lax.rem(me + turn, size_px)).wait_send()
+
+        @pl.loop(1, half)
+        def _(turn):
             for slot in range(slots):
-                back(slot, chunk, me, peer).wait_send()
-                back(slot, chunk, peer, me).wait_recv()
+                back(slot, chunk, me, mate(turn)).wait_send()
+                back(slot, chunk, mate(turn), me).wait_recv()
+
+    @pl.when(before >= half)
+    def _():
+        plane(0, 0, before).wait_send()
+
+    @pl.when(me == half)
+    def _():
+        plane(1, 1, 0).wait_send()
+        plane(1, 2, size_px - 1).wait_send()
 
     for home in homes:
         home.wait()
+
+
+def paired_order(length):
+    counter = np.arange(length // 2)
+    mirror = np.where(counter == 0, length // 2, length - counter)
+    return np.stack([counter, mirror], axis=1).reshape(-1)
 
 
 def kernel_path(adjoint, saved, spectra, chosen):
@@ -273,7 +354,10 @@
     f32 = jnp.float32
     block = 8
     right_three = as_three(hartley(three), 0)
-    left_two, left_one = as_three(hartley(two), 1), as_three(hartley(one), 1)
+    order, half = paired_order(two), size_px // 2
+    left_two = as_three(hartley(two)[order], 1)
+    left_two_back = as_three(hartley(two)[:, order], 1)
+    left_one = as_three(hartley(one), 1)
 
     field = pl.pallas_call(
         third_kernel,
@@ -292,28 +376,30 @@
             pl.BlockSpec((size_py, block, lines, width), lambda i: (0, i, 0, 0)),
             whole(left_two),
         ],
-        out_specs=pl.BlockSpec((size_px, local, block, width), lambda i: (0, 0, i, 0)),
-        out_shape=jax.ShapeDtypeStruct((size_px, local, planes, width), f32),
+        out_specs=pl.BlockSpec((half, 2 * local, block, width), lambda i: (0, 0, i, 0)),
+        out_shape=jax.ShapeDtypeStruct((half, 2 * local, planes, width), f32),
         scratch_shapes=[pltpu.VMEM((block, two, width), f32)],
         compiler_params=params(),
         name="second",
     )(field, left_two)
-    chunks = 4
+    chunks = 8
     dma = pltpu.SemaphoreType.DMA
     field = pl.pallas_call(
         functools.partial(middle_kernel, chunks),
         in_specs=[anywhere, anywhere, pl.BlockSpec(memory_space=pltpu.VMEM)],
         out_specs=anywhere,
-        out_shape=jax.ShapeDtypeStruct((slots, size_px, local, planes, width), f32),
+        out_shape=jax.ShapeDtypeStruct((slots, half, 2 * local, planes, width), f32),
         scratch_shapes=[
-            pltpu.VMEM((size_px, local, planes, width), f32),
+            pltpu.VMEM((size_px, 2 * local, planes, width), f32),
             pltpu.VMEM((slots, one, local, width), spectra.dtype),
-            pltpu.VMEM((slots, local, one, width), f32),
-            pltpu.VMEM((slots, size_px, local, planes, width), f32),
+            pltpu.VMEM((slots, local + 2, one, width), f32),
+            pltpu.VMEM((slots, half, 2 * local, planes, width), f32),
             dma((chunks, size_px)),
             dma((chunks, size_px)),
-            dma((slots, chunks, size_px)),
-            dma((slots, chunks, size_px)),
+            dma((slots, chunks, half)),
+            dma((slots, chunks, half)),
+            dma((3,)),
+            dma((2,)),
             dma,
             dma((slots,)),
             dma,
@@ -325,15 +411,15 @@
         second_back_kernel,
         grid=(slots, planes // block),
         in_specs=[
-            pl.BlockSpec((1, size_px, local, block, width), lambda j, i: (j, 0, 0, i, 0)),
-            whole(left_two),
+            pl.BlockSpec((1, half, 2 * local, block, width), lambda j, i: (j, 0, 0, i, 0)),
+            whole(left_two_back),
         ],
         out_specs=pl.BlockSpec((size_py, 1, block, lines, width), lambda j, i: (0, j, i, 0, 0)),
         out_shape=jax.ShapeDtypeStruct((size_py, slots, planes, lines, width), f32),
         scratch_shapes=[pltpu.VMEM((block, two, width), f32)],
         compiler_params=params(),
         name="second_back",
-    )(field, left_two)
+    )(field, left_two_back)
     field = lax.all_to_all(field, "py", split_axis=0, concat_axis=0, tiled=True)
     scale = 1.0 / (one * two * three)
     piece = 4
@@ -356,7 +442,8 @@
 def on_device(adjoint, saved, spectra, freq_index, picked):
     chosen = chosen_index(freq_index, picked)
     width = adjoint.shape[2] // lax.axis_size("py")
-    if adjoint.shape[0] % 8 == 0 and spectra.shape[2] % 8 == 0 and width % 128 == 0:
+    even = lax.axis_size("px") % 2 == 0
+    if even and adjoint.shape[0] % 8 == 0 and spectra.shape[2] % 8 == 0 and width % 128 == 0:
         return kernel_path(adjoint, saved, spectra, chosen)
     return plain_path(adjoint, saved, spectra, chosen)
 

time: 342 us -> 310 us (0.906)
  the two profiles are of different devices: /device:TPU:11 before, /device:TPU:0 now
where the time goes in v3:
time: 310 us; the launch traced here: 309 us
  Pallas kernels  282 us (91%)
  blocking collectives  11.9 us (4%)
  starting transfers between devices  7.08 us (2%)
  waiting for transfers between devices  6.73 us (2%)
    pallas_call x1, Pallas kernels, kernel_path(): pl.pallas_call(functools.partial(middle_kernel, chunks), in_specs=[anywhe...  246 us
    pallas_call x1, Pallas kernels, kernel_path(): pl.pallas_call(functools.partial(third_back_kernel, scale), grid=(planes...  13.7 us
    all_to_all x1, blocking collectives, kernel_path(): field = lax.all_to_all(field, 'py', split_axis=0, concat_axis=0, tiled=True)  11.9 us
    pallas_call x1, Pallas kernels, kernel_path(): pl.pallas_call(second_back_kernel, grid=(slots, planes // block), in_spec...  10.7 us
    all_to_all x1, starting transfers between devices, kernel_path(): field = lax.all_to_all(field, 'py', split_axis=0, concat_axis=0, tiled=True)  7.08 us
    all_to_all x1, waiting for transfers between devices, kernel_path(): field = lax.all_to_all(field, 'py', split_axis=0, concat_axis=0, tiled=True)  6.73 us
  transfers between devices with their start and end apart: 1, of which 1 were waited for; matrix products, arithmetic and copies ran while one was open for 0% of the time, Pallas kernels for 0%

profile of v3, /device:TPU:0, one launch (start us, length us, event | category | flops | bytes accessed | tf_op | source)
XLA Modules:
  0.0 308.7 jit_solution(9305498487635033797)
XLA Ops:
  0.0 5.9 %third.1 = f32[2,32,128,128]{3,2,1,0:T(8,128)} custom-call(f32[32,128,256]{2,1,0:T(8,128)} %field_ref.1, bf16[768,256]{1,0:T(8,128)(2,1)} %constant.10.clone.table_ref), custom_call_target="tpu_custom_call" | custom-call | tf_op jit(solution)/shard_map/third/pallas_call | solution.py:362
  5.9 11.9 %all_to_all.10.field_ref = f32[2,32,128,128]{3,2,1,0:T(8,128)} all-to-all(f32[2,32,128,128]{3,2,1,0:T(8,128)} %third.1), channel_id=1, replica_groups=mesh['chain'=2,'px'=8,'py'=2] {'py'}, dimensions={0} | all-to-all | bytes 8388608 | tf_op jit(solution)/shard_map/all_to_all | solution.py:371
  17.8 5.9 %second.1.field_ref = f32[4,64,32,128]{3,2,1,0:T(8,128)} custom-call(f32[2,32,128,128]{3,2,1,0:T(8,128)} %all_to_all.10.field_ref, bf16[256,768]{1,0:T(8,128)(2,1)} %constant.11.clone.table_ref), custom_call_target="tpu_custom_call" | custom-call | tf_op jit(solution)/shard_map/second/pallas_call | solution.py:372
  23.7 245.9 %middle.1.field_ref = f32[2,4,64,32,128]{4,3,2,1,0:T(8,128)} custom-call(f32[4,64,32,128]{3,2,1,0:T(8,128)} %second.1.field_ref, bf16[2,256,32,256]{3,2,1,0:T(8,128)(2,1)} %spectra_ref.1, bf16[256,768]{1,0:T(8,128)(2,1)} %constant.13.clone.table_ref), custom_call_target="tpu_custom_call" | custom-call | tf_op jit(solution)/shard_map/middle/pallas_call | solution.py:387
  269.6 10.7 %second_back.1 = f32[2,2,32,128,128]{4,3,2,1,0:T(8,128)} custom-call(f32[2,4,64,32,128]{4,3,2,1,0:T(8,128)} %middle.1.field_ref, bf16[256,768]{1,0:T(8,128)(2,1)} %constant.12.clone.table_ref), custom_call_target="tpu_custom_call" | custom-call | tf_op jit(solution)/shard_map/second_back/pallas_call | solution.py:410
  280.3 0.0 copy-start
  280.3 0.0 copy-start.1
  280.3 7.1 %all-to-all-start.1 = ((f32[2,2,32,128,128]{4,3,2,1,0:T(8,128)}), f32[2,2,32,128,128]{4,3,2,1,0:T(8,128)}, u32[]{:S(2)}, u32[]{:S(2)}) async-start(f32[2,2,32,128,128]{4,3,2,1,0:T(8,128)} %second_back.1), calls=%async_computation.1 | async-start | bytes 16777216 | tf_op jit(solution)/shard_map/all_to_all | solution.py:423
  287.4 0.0 copy-done
  287.4 0.0 copy-done.1
  287.5 0.7 fusion.chosen_ref
  288.2 6.7 %all-to-all-done.1.field_ref = f32[2,2,32,128,128]{4,3,2,1,0:T(8,128)} async-done(((f32[2,2,32,128,128]{4,3,2,1,0:T(8,128)}), f32[2,2,32,128,128]{4,3,2,1,0:T(8,128)}, u32[]{:S(2)}, u32[]{:S(2)}) %all-to-all-start.1) | async-done | bytes 8388640 | tf_op jit(solution)/shard_map/all_to_all | solution.py:423
  294.9 13.7 %third_back.1 = f32[32,128,256]{2,1,0:T(8,128)} custom-call(s32[2]{0:T(128)} %fusion.chosen_ref, f32[2,2,32,128,128]{4,3,2,1,0:T(8,128)} %all-to-all-done.1.field_ref, f32[32,128,256]{2,1,0:T(8,128)} %saved_ref.1, bf16[768,256]{1,0:T(8,128)(2,1)} %constant.10.clone.table_ref), custom_call_target="tpu_custom_call" | custom-call | tf_op jit(solution)/shard_map/third_back/pallas_call | solution.py:426
Async XLA Ops:
  280.3 7.1 %copy-start = (s32[8]{0:T(128)S(1)}, s32[8]{0:T(128)}, u32[]{:S(2)}) copy-start(s32[8]{0:T(128)} %param.12) | copy-start | bytes 100
  280.3 7.1 %copy-start.1 = (s32[2]{0:T(128)S(1)}, s32[2]{0:T(128)}, u32[]{:S(2)}) copy-start(s32[2]{0:T(128)} %param.13) | copy-start | bytes 28
  280.3 14.6 %all-to-all-start.1 = ((f32[2,2,32,128,128]{4,3,2,1,0:T(8,128)}), f32[2,2,32,128,128]{4,3,2,1,0:T(8,128)}, u32[]{:S(2)}, u32[]{:S(2)}) async-start(f32[2,2,32,128,128]{4,3,2,1,0:T(8,128)} %second_back.1), calls=%async_computation.1 | async-start | bytes 16777216 | tf_op jit(solution)/shard_map/all_to_all | solution.py:423

commit v4 on v3

--- a/solution.py
+++ b/solution.py
@@ -74,13 +74,65 @@
     return pltpu.CompilerParams(vmem_limit_bytes=58 << 20, **more)
 
 
-def third_kernel(field_ref, table_ref, out_ref):
+def core_exchange(step, steps, source, target, sems):
+    send_sem, recv_sem, own_sem = sems
+    me = lax.axis_index("py")
+    other = 1 - me
+
+    def away(at, sender, receiver):
+        return pltpu.make_async_remote_copy(
+            src_ref=source(receiver, at),
+            dst_ref=target(sender, at),
+            send_sem=send_sem.at[at],
+            recv_sem=recv_sem.at[at],
+            device_id={"py": receiver},
+            device_id_type=pl.DeviceIdType.MESH,
+        )
+
+    def stay(at):
+        return pltpu.make_async_copy(source(me, at), target(me, at), own_sem.at[at])
+
+    away(step, me, other).start()
+    stay(step).start()
+
+    @pl.when(step == steps - 1)
+    def _():
+        @pl.loop(0, steps)
+        def _(at):
+            away(at, me, other).wait_send()
+            away(at, other, me).wait_recv()
+            stay(at).wait()
+
+
+def greet_core():
+    barrier = pltpu.get_barrier_semaphore()
+    other = 1 - lax.axis_index("py")
+    pl.semaphore_signal(
+        barrier, inc=1, device_id={"py": other}, device_id_type=pl.DeviceIdType.MESH
+    )
+    pl.semaphore_wait(barrier, 1)
+
+
+def third_kernel(steps, field_ref, table_ref, out_ref, mine, *sems):
     planes, lines, three = field_ref.shape
-    parts, _, _, width = out_ref.shape
+    parts, width = mine.shape[0], mine.shape[3]
+    step = pl.program_id(0)
+    pl.when(step == 0)(greet_core)
+
+    def rows(at):
+        return pl.ds(pl.multiple_of(at * planes, planes), planes)
+
     result = from_right(field_ref[...].reshape(planes * lines, three), table_ref[...])
     for part in range(parts):
         piece = result[:, part * width : (part + 1) * width]
-        out_ref[part] = piece.reshape(planes, lines, width)
+        mine[part, rows(step)] = piece.reshape(planes, lines, width)
+    core_exchange(
+        step,
+        steps,
+        lambda part, at: mine.at[part, rows(at)],
+        lambda part, at: out_ref.at[part, rows(at)],
+        sems,
+    )
 
 
 def second_kernel(field_ref, table_ref, out_ref, held):
@@ -98,18 +150,28 @@
         out_ref[peer] = jnp.swapaxes(held[:, peer * local : (peer + 1) * local, :], 0, 1)
 
 
-def second_back_kernel(field_ref, table_ref, out_ref, held):
-    _, size_px, local, planes, width = field_ref.shape
-    parts, _, _, lines, _ = out_ref.shape
-    for peer in range(size_px):
-        held[:, peer * local : (peer + 1) * local, :] = jnp.swapaxes(field_ref[0, peer], 0, 1)
+def second_back_kernel(steps, field_ref, table_ref, out_ref, held, mine, *sems):
+    _, groups, local, planes, width = field_ref.shape
+    parts, lines = mine.shape[0], mine.shape[3]
+    inner = steps // mine.shape[1]
+    step = pl.program_id(0) * inner + pl.program_id(1)
+    slot = pl.program_id(0)
+    begin = pl.program_id(1) * planes
+    pl.when(step == 0)(greet_core)
+    for group in range(groups):
+        held[:, group * local : (group + 1) * local, :] = jnp.swapaxes(field_ref[0, group], 0, 1)
     for plane in range(0, planes, 2):
         columns = jnp.concatenate([held[plane], held[plane + 1]], axis=1)
         result = from_left(table_ref[...], columns)
         for part in range(parts):
             rows = result[part * lines : (part + 1) * lines]
-            out_ref[part, 0, plane] = rows[:, :width]
-            out_ref[part, 0, plane + 1] = rows[:, width:]
+            mine[part, slot, begin + plane] = rows[:, :width]
+            mine[part, slot, begin + plane + 1] = rows[:, width:]
+
+    def block(ref):
+        return lambda part, at: ref.at[part, at // inner, pl.ds((at % inner) * planes, planes)]
+
+    core_exchange(step, steps, block(mine), block(out_ref), sems)
 
 
 def cosine_turns(turns):
@@ -353,6 +415,8 @@
     anywhere = pl.BlockSpec(memory_space=pl.ANY)
     f32 = jnp.float32
     block = 8
+    steps = planes // block
+    dma = pltpu.SemaphoreType.DMA
     right_three = as_three(hartley(three), 0)
     order, half = paired_order(two), size_px // 2
     left_two = as_three(hartley(two)[order], 1)
@@ -360,15 +424,15 @@
     left_one = as_three(hartley(one), 1)
 
     field = pl.pallas_call(
-        third_kernel,
-        grid=(planes // block,),
+        functools.partial(third_kernel, steps),
+        grid=(steps,),
         in_specs=[pl.BlockSpec((block, lines, three), lambda i: (i, 0, 0)), whole(right_three)],
-        out_specs=pl.BlockSpec((size_py, block, lines, width), lambda i: (0, i, 0, 0)),
+        out_specs=anywhere,
         out_shape=jax.ShapeDtypeStruct((size_py, planes, lines, width), f32),
-        compiler_params=params(),
+        scratch_shapes=[pltpu.VMEM((size_py, planes, lines, width), f32)] + [dma((steps,))] * 3,
+        compiler_params=params(collective_id=1, has_side_effects=True),
         name="third",
     )(adjoint, right_three)
-    field = lax.all_to_all(field, "py", split_axis=0, concat_axis=0, tiled=True)
     field = pl.pallas_call(
         second_kernel,
         grid=(planes // block,),
@@ -383,7 +447,6 @@
         name="second",
     )(field, left_two)
     chunks = 8
-    dma = pltpu.SemaphoreType.DMA
     field = pl.pallas_call(
         functools.partial(middle_kernel, chunks),
         in_specs=[anywhere, anywhere, pl.BlockSpec(memory_space=pltpu.VMEM)],
@@ -408,19 +471,22 @@
         name="middle",
     )(field, spectra, left_one)
     field = pl.pallas_call(
-        second_back_kernel,
-        grid=(slots, planes // block),
+        functools.partial(second_back_kernel, slots * steps),
+        grid=(slots, steps),
         in_specs=[
             pl.BlockSpec((1, half, 2 * local, block, width), lambda j, i: (j, 0, 0, i, 0)),
             whole(left_two_back),
         ],
-        out_specs=pl.BlockSpec((size_py, 1, block, lines, width), lambda j, i: (0, j, i, 0, 0)),
+        out_specs=anywhere,
         out_shape=jax.ShapeDtypeStruct((size_py, slots, planes, lines, width), f32),
-        scratch_shapes=[pltpu.VMEM((block, two, width), f32)],
-        compiler_params=params(),
+        scratch_shapes=[
+            pltpu.VMEM((block, two, width), f32),
+            pltpu.VMEM((size_py, slots, planes, lines, width), f32),
+        ]
+        + [dma((slots * steps,))] * 3,
+        compiler_params=params(collective_id=2, has_side_effects=True),
         name="second_back",
     )(field, left_two_back)
-    field = lax.all_to_all(field, "py", split_axis=0, concat_axis=0, tiled=True)
     scale = 1.0 / (one * two * three)
     piece = 4
     return pl.pallas_call(
@@ -442,7 +508,7 @@
 def on_device(adjoint, saved, spectra, freq_index, picked):
     chosen = chosen_index(freq_index, picked)
     width = adjoint.shape[2] // lax.axis_size("py")
-    even = lax.axis_size("px") % 2 == 0
+    even = lax.axis_size("px") % 2 == 0 and lax.axis_size("py") == 2
     if even and adjoint.shape[0] % 8 == 0 and spectra.shape[2] % 8 == 0 and width % 128 == 0:
         return kernel_path(adjoint, saved, spectra, chosen)
     return plain_path(adjoint, saved, spectra, chosen)

time: 310 us -> 285 us (0.919)
  blocking collectives: 11.9 us -> 0 us
  starting transfers between devices: 7.08 us -> 0 us
  waiting for transfers between devices: 6.73 us -> 0 us
    all_to_all x1 -> x0, blocking collectives: 11.9 us -> none  [kernel_path(): field = lax.all_to_all(field, 'py', split_axis=0, concat_axis=0, tiled=True)]
    all_to_all x1 -> x0, starting transfers between devices: 7.08 us -> none  [kernel_path(): field = lax.all_to_all(field, 'py', split_axis=0, concat_axis=0, tiled=True)]
    all_to_all x1 -> x0, waiting for transfers between devices: 6.73 us -> none  [kernel_path(): field = lax.all_to_all(field, 'py', split_axis=0, concat_axis=0, tiled=True)]
  transfers between devices with their start and end apart: 1 -> 0, of which waited for: 1 -> 0; matrix products, arithmetic and copies ran while one was open for 0% -> 0% of each run, Pallas kernels for 0% -> 0%
where the time goes in v4:
time: 285 us
  Pallas kernels  284 us (100%)
    pallas_call x1, Pallas kernels, kernel_path(): pl.pallas_call(functools.partial(middle_kernel, chunks), in_specs=[anywhe...  246 us
    pallas_call x1, Pallas kernels, kernel_path(): pl.pallas_call(functools.partial(third_back_kernel, scale), grid=(planes...  13.7 us
    pallas_call x1, Pallas kernels, kernel_path(): pl.pallas_call(functools.partial(second_back_kernel, slots * steps), grid...  11.4 us
    pallas_call x1, Pallas kernels, kernel_path(): pl.pallas_call(functools.partial(third_kernel, steps), grid=(steps,), in_...  6.93 us
    pallas_call x1, Pallas kernels, kernel_path(): pl.pallas_call(second_kernel, grid=(planes // block,), in_specs=[pl.Block...  5.97 us

profile of v4, /device:TPU:0, one launch (start us, length us, event | category | flops | bytes accessed | tf_op | source)
XLA Modules:
  0.0 284.5 jit_solution(10554497811286564924)
XLA Ops:
  0.0 6.9 %third.1.field_ref = f32[2,32,128,128]{3,2,1,0:T(8,128)} custom-call(f32[32,128,256]{2,1,0:T(8,128)} %field_ref.1, bf16[768,256]{1,0:T(8,128)(2,1)} %constant.10.clone.table_ref), custom_call_target="tpu_custom_call" | custom-call | tf_op jit(solution)/shard_map/third/pallas_call | solution.py:426
  6.9 6.0 %second.1.field_ref = f32[4,64,32,128]{3,2,1,0:T(8,128)} custom-call(f32[2,32,128,128]{3,2,1,0:T(8,128)} %third.1.field_ref, bf16[256,768]{1,0:T(8,128)(2,1)} %constant.11.clone.table_ref), custom_call_target="tpu_custom_call" | custom-call | tf_op jit(solution)/shard_map/second/pallas_call | solution.py:436
  12.9 245.8 %middle.1.field_ref = f32[2,4,64,32,128]{4,3,2,1,0:T(8,128)} custom-call(f32[4,64,32,128]{3,2,1,0:T(8,128)} %second.1.field_ref, bf16[2,256,32,256]{3,2,1,0:T(8,128)(2,1)} %spectra_ref.1, bf16[256,768]{1,0:T(8,128)(2,1)} %constant.13.clone.table_ref), custom_call_target="tpu_custom_call" | custom-call | tf_op jit(solution)/shard_map/middle/pallas_call | solution.py:450
  258.7 0.0 copy-start
  258.7 0.0 copy-start.1
  258.7 11.4 %second_back.1.field_ref = f32[2,2,32,128,128]{4,3,2,1,0:T(8,128)} custom-call(f32[2,4,64,32,128]{4,3,2,1,0:T(8,128)} %middle.1.field_ref, bf16[256,768]{1,0:T(8,128)(2,1)} %constant.12.clone.table_ref), custom_call_target="tpu_custom_call" | custom-call | tf_op jit(solution)/shard_map/second_back/pallas_call | solution.py:473
  270.1 0.0 copy-done
  270.1 0.0 copy-done.1
  270.1 0.7 fusion.chosen_ref
  270.8 13.7 %third_back.1 = f32[32,128,256]{2,1,0:T(8,128)} custom-call(s32[2]{0:T(128)} %fusion.chosen_ref, f32[2,2,32,128,128]{4,3,2,1,0:T(8,128)} %second_back.1.field_ref, f32[32,128,256]{2,1,0:T(8,128)} %saved_ref.1, bf16[768,256]{1,0:T(8,128)(2,1)} %constant.10.clone.table_ref), custom_call_target="tpu_custom_call" | custom-call | tf_op jit(solution)/shard_map/third_back/pallas_call | solution.py:492
Async XLA Ops:
  258.7 11.4 %copy-start = (s32[8]{0:T(128)S(1)}, s32[8]{0:T(128)}, u32[]{:S(2)}) copy-start(s32[8]{0:T(128)} %param.12) | copy-start | bytes 100
  258.7 11.4 %copy-start.1 = (s32[2]{0:T(128)S(1)}, s32[2]{0:T(128)}, u32[]{:S(2)}) copy-start(s32[2]{0:T(128)} %param.13) | copy-start | bytes 28
